TPU v7x, 32 devices: a whole 2x2x4 slice. The times are simulated.
32 devices in a mesh: fsdp: 16 (over z, x, core), heads: 2 (over y).
Axes of the slice: x: 2, y: 2, z: 4, core: 2. Of those that a mesh axis runs over, the one named last changes fastest.
Arguments:
- tokens: bfloat16 [24576, 1280], P(('fsdp', 'heads')), may hold values from -6 to 6
- w_query: bfloat16 [1280, 1280], P('fsdp', 'heads'), may hold values from -0.15625 to 0.15625
- w_key: bfloat16 [1280, 1280], P('fsdp', 'heads'), may hold values from -0.15625 to 0.15625
- w_value: bfloat16 [1280, 1280], P('fsdp', 'heads'), may hold values from -0.15625 to 0.15625
- w_output: bfloat16 [1280, 1280], P('heads', 'fsdp'), may hold values from -0.25 to 0.25
- w_hidden: bfloat16 [1280, 1280], P('fsdp', 'heads'), may hold values from -0.15625 to 0.15625
- bias_hidden: bfloat16 [1280], P(('heads', 'fsdp')), may hold values from -3 to 3
- w_project: bfloat16 [1280, 1280], P('heads', 'fsdp'), may hold values from -0.25 to 0.25
- bias_output: bfloat16 [1280], P(('heads', 'fsdp')), may hold values from -3 to 3
- gain_first: bfloat16 [1280], P(('heads', 'fsdp')), may hold values from 0.099609375 to 1.8984375
- gain_second: bfloat16 [1280], P(('heads', 'fsdp')), may hold values from 0.099609375 to 1.8984375
- lengths: int32 [48, 160], P('fsdp'), may hold values from 1 to 64, 512 in all within a row
- cotangent: bfloat16 [24576, 1280], P(('fsdp', 'heads')), may hold values from -6 to 6
Outputs:
- mixed: bfloat16 [24576, 1280], P(('fsdp', 'heads'))
- grad_tokens: bfloat16 [24576, 1280], P(('fsdp', 'heads'))
- grad_query: float32 [1280, 1280], P('fsdp', 'heads')
- grad_key: float32 [1280, 1280], P('fsdp', 'heads')
- grad_value: float32 [1280, 1280], P('fsdp', 'heads')
- grad_output: float32 [1280, 1280], P('heads', 'fsdp')
- grad_hidden: float32 [1280, 1280], P('fsdp', 'heads')
- grad_hidden_bias: float32 [1280], P(('heads', 'fsdp'))
- grad_project: float32 [1280, 1280], P('heads', 'fsdp')
- grad_output_bias: float32 [1280], P(('heads', 'fsdp'))
- grad_gain_first: float32 [1280], P(('heads', 'fsdp'))
- grad_gain_second: float32 [1280], P(('heads', 'fsdp'))
Inputs may be any that keep to these rules, and one draw needn't show every extreme that they name: Each row's 160 lengths sum to 512; every row has a series of exactly 64 patches.
All inputs are finite; a program needn't handle non-finite values.
Results may differ from a plain program's by a relative error of at most 0.022.
Values may be sent and summed in bfloat16 or wider, within the bound.
No kernel may reach another device: no remote copies, remote signals or barrier semaphores. Data moves between devices by JAX's collectives and lax.ppermute only.
A program may use at most 192 MiB of HBM per device.

v0:
```python
from functools import partial
import math

import jax
import jax.numpy as jnp
from jax import lax
from jax.sharding import PartitionSpec as P

HEAD_DIM = 80
ROW = 512


EPS = 1e-06
NEG = -1e30
THETA = 10000.0


def tables(lengths_row):
    ends = jnp.cumsum(lengths_row, dtype=jnp.int32)
    place = jnp.arange(ROW, dtype=jnp.int32)
    done = ends[None, :] <= place[:, None]
    series = jnp.sum(done.astype(jnp.int32), axis=1, dtype=jnp.int32)
    offset = jnp.sum(jnp.where(done, lengths_row[None, :], 0), axis=1, dtype=jnp.int32)
    position = (place - offset).astype(jnp.float32)
    allowed = (series[:, None] == series[None, :]) & (place[None, :] <= place[:, None])
    half = HEAD_DIM // 2
    freq = jnp.exp(-jnp.arange(half, dtype=jnp.float32) * (2.0 * math.log(THETA) / HEAD_DIM))
    angle = position[:, None] * freq[None, :]
    return (allowed, jnp.cos(angle), jnp.sin(angle))


def turn(vectors, cosine, sine):
    half = vectors.shape[-1] // 2
    first = vectors[..., :half]
    second = vectors[..., half:]
    return jnp.concatenate(
        [first * cosine - second * sine, second * cosine + first * sine], axis=-1
    )


def turn_back(vectors, cosine, sine):
    half = vectors.shape[-1] // 2
    first = vectors[..., :half]
    second = vectors[..., half:]
    return jnp.concatenate(
        [first * cosine + second * sine, second * cosine - first * sine], axis=-1
    )


def contract_first(left, right):
    return lax.dot_general(
        left, right, (((0,), (0,)), ((), ())), preferred_element_type=jnp.float32
    )


def contract_last(left, right):
    return lax.dot_general(
        left, right, (((1,), (1,)), ((), ())), preferred_element_type=jnp.float32
    )


def norm_back(grad_norm, source, factor, gain):
    scaled = gain * grad_norm
    inner = jnp.mean(scaled * source, axis=1, keepdims=True)
    grad_source = factor * scaled - source * (factor * factor * factor) * inner
    return (grad_source, jnp.sum(grad_norm * source * factor, axis=0))


def attend_row(item):
    queries, keys, values, allowed = item
    scores = jnp.einsum(
        "qhd,khd->hqk", queries, keys, preferred_element_type=jnp.float32
    ) * HEAD_DIM ** (-0.5)
    scores = jnp.where(allowed[None], scores, NEG)
    peak = jnp.max(scores, axis=-1, keepdims=True)
    expo = jnp.exp(scores - peak)
    total = jnp.sum(expo, axis=-1, keepdims=True)
    weights = (expo / total).astype(jnp.bfloat16)
    result = jnp.einsum("hqk,khd->qhd", weights, values, preferred_element_type=jnp.float32).astype(
        jnp.bfloat16
    )
    return (result, (peak + jnp.log(total))[..., 0])


def attend_back_row(item):
    queries, keys, values, allowed, logsum, grad_out = item
    scale = HEAD_DIM ** (-0.5)
    scores = jnp.einsum("qhd,khd->hqk", queries, keys, preferred_element_type=jnp.float32) * scale
    scores = jnp.where(allowed[None], scores, NEG)
    probs = jnp.exp(scores - logsum[..., None])
    weights = probs.astype(jnp.bfloat16)
    grad_values = jnp.einsum(
        "hqk,qhd->khd", weights, grad_out, preferred_element_type=jnp.float32
    ).astype(jnp.bfloat16)
    grad_probs = jnp.einsum("qhd,khd->hqk", grad_out, values, preferred_element_type=jnp.float32)
    grad_scores = (
        probs * (grad_probs - jnp.sum(probs * grad_probs, axis=-1, keepdims=True))
    ).astype(jnp.bfloat16)
    grad_queries = (
        jnp.einsum("hqk,khd->qhd", grad_scores, keys, preferred_element_type=jnp.float32) * scale
    )
    grad_keys = (
        jnp.einsum("hqk,qhd->khd", grad_scores, queries, preferred_element_type=jnp.float32) * scale
    )
    return (grad_queries, grad_keys, grad_values)


def local(
    tokens,
    w_query,
    w_key,
    w_value,
    w_output,
    w_hidden,
    bias_hidden,
    w_project,
    bias_output,
    gain_first,
    gain_second,
    lengths,
    cotangent,
):
    gathered = (
        lax.all_gather(w_query, "fsdp", axis=0, tiled=True),
        lax.all_gather(w_key, "fsdp", axis=0, tiled=True),
        lax.all_gather(w_value, "fsdp", axis=0, tiled=True),
        lax.all_gather(w_output, "fsdp", axis=1, tiled=True),
        lax.all_gather(w_hidden, "fsdp", axis=0, tiled=True),
        lax.all_gather(w_project, "fsdp", axis=1, tiled=True),
        lax.all_gather(bias_hidden, "fsdp", axis=0, tiled=True),
        lax.all_gather(bias_output, "fsdp", axis=0, tiled=True),
        lax.all_gather(gain_first, "fsdp", axis=0, tiled=True),
        lax.all_gather(gain_second, "fsdp", axis=0, tiled=True),
    )
    (
        full_query,
        full_key,
        full_value,
        full_output,
        full_hidden,
        full_project,
        hidden_shift,
        output_part,
        first_cols,
        second_cols,
    ) = gathered
    rows_whole, gain_one, gain_two, output_shift = (
        lax.all_gather(tokens, "heads", axis=0, tiled=True),
        lax.all_gather(first_cols, "heads", axis=0, tiled=True),
        lax.all_gather(second_cols, "heads", axis=0, tiled=True),
        lax.all_gather(output_part, "heads", axis=0, tiled=True),
    )
    source = rows_whole.astype(jnp.float32)
    gain_one = gain_one.astype(jnp.float32)
    gain_two = gain_two.astype(jnp.float32)
    row_count = lengths.shape[0]
    local_heads = full_query.shape[1] // HEAD_DIM
    allowed, cosine, sine = jax.vmap(tables)(lengths)
    cos_heads = cosine[:, :, None, :]
    sin_heads = sine[:, :, None, :]
    own_rows = tokens.shape[0]
    row_start = lax.axis_index("heads") * own_rows
    factor_one = lax.rsqrt(jnp.mean(source * source, axis=1, keepdims=True) + EPS)
    normed = (source * factor_one * gain_one).astype(jnp.bfloat16)

    def split_heads(weight):
        return jnp.dot(normed, weight, preferred_element_type=jnp.float32).reshape(
            row_count, ROW, local_heads, HEAD_DIM
        )

    queries = turn(split_heads(full_query), cos_heads, sin_heads).astype(jnp.bfloat16)
    keys = turn(split_heads(full_key), cos_heads, sin_heads).astype(jnp.bfloat16)
    values = split_heads(full_value).astype(jnp.bfloat16)
    heads_out, logsum = lax.map(attend_row, (queries, keys, values, allowed))
    attended = heads_out.reshape(row_count * ROW, local_heads * HEAD_DIM)
    branch = jnp.dot(attended, full_output, preferred_element_type=jnp.float32)
    resid = source + lax.psum(branch.astype(jnp.bfloat16), "heads").astype(jnp.float32)
    factor_two = lax.rsqrt(jnp.mean(resid * resid, axis=1, keepdims=True) + EPS)
    second = (resid * factor_two * gain_two).astype(jnp.bfloat16)
    resid_local = lax.dynamic_slice_in_dim(resid, row_start, own_rows, 0)
    hidden = jnp.dot(second, full_hidden, preferred_element_type=jnp.float32) + hidden_shift.astype(
        jnp.float32
    )
    active_full, gelu_pull = jax.vjp(partial(jax.nn.gelu, approximate=True), hidden)
    active = active_full.astype(jnp.bfloat16)
    feed = jnp.dot(active, full_project, preferred_element_type=jnp.float32)
    feed_local = lax.psum_scatter(
        feed.astype(jnp.bfloat16), "heads", scatter_dimension=0, tiled=True
    ).astype(jnp.float32)
    mixed = (resid_local + feed_local + output_shift.astype(jnp.float32)[None, :]).astype(
        jnp.bfloat16
    )
    again = (
        lax.all_gather(w_query, "fsdp", axis=0, tiled=True),
        lax.all_gather(w_key, "fsdp", axis=0, tiled=True),
        lax.all_gather(w_value, "fsdp", axis=0, tiled=True),
        lax.all_gather(w_output, "fsdp", axis=1, tiled=True),
        lax.all_gather(w_hidden, "fsdp", axis=0, tiled=True),
        lax.all_gather(w_project, "fsdp", axis=1, tiled=True),
    )
    back_query, back_key, back_value, back_output, back_hidden, back_project = again
    grad_whole = lax.all_gather(cotangent, "heads", axis=0, tiled=True)
    grad_local = cotangent.astype(jnp.float32)
    col_width = output_part.shape[0]
    col_start = lax.axis_index("heads") * col_width
    grad_output_bias = jnp.sum(
        lax.dynamic_slice_in_dim(grad_whole, col_start, col_width, 1).astype(jnp.float32), axis=0
    )
    grad_project = contract_first(active, grad_whole)
    grad_active = contract_last(grad_whole, back_project)
    grad_pre = gelu_pull(grad_active)[0].astype(jnp.bfloat16)
    grad_hidden_bias = jnp.sum(grad_pre.astype(jnp.float32), axis=0)
    grad_hidden = contract_first(second, grad_pre)
    grad_second = contract_last(grad_pre, back_hidden)
    resid_term, second_gain_part = norm_back(grad_second, resid, factor_two, gain_two)
    resid_norm, second_gain_cols = (
        lax.psum_scatter(
            resid_term.astype(jnp.bfloat16), "heads", scatter_dimension=0, tiled=True
        ).astype(jnp.float32),
        lax.psum_scatter(
            second_gain_part.astype(jnp.bfloat16), "heads", scatter_dimension=0, tiled=True
        ).astype(jnp.float32),
    )
    grad_resid = grad_local + resid_norm
    grad_branch = lax.all_gather(grad_resid.astype(jnp.bfloat16), "heads", axis=0, tiled=True)
    grad_output = contract_first(attended, grad_branch)
    grad_attended = contract_last(grad_branch, back_output).astype(jnp.bfloat16)
    grad_heads = grad_attended.reshape(row_count, ROW, local_heads, HEAD_DIM)
    grad_queries, grad_keys, grad_values = lax.map(
        attend_back_row, (queries, keys, values, allowed, logsum, grad_heads)
    )
    flat = (row_count * ROW, local_heads * HEAD_DIM)
    grad_queries = turn_back(grad_queries, cos_heads, sin_heads).astype(jnp.bfloat16).reshape(flat)
    grad_keys = turn_back(grad_keys, cos_heads, sin_heads).astype(jnp.bfloat16).reshape(flat)
    grad_values = grad_values.reshape(flat)
    grad_query = contract_first(normed, grad_queries)
    grad_key = contract_first(normed, grad_keys)
    grad_value = contract_first(normed, grad_values)
    grad_normed = (
        contract_last(grad_queries, back_query)
        + contract_last(grad_keys, back_key)
        + contract_last(grad_values, back_value)
    )
    source_term, first_gain_part = norm_back(grad_normed, source, factor_one, gain_one)
    source_norm, first_gain_cols = (
        lax.psum_scatter(
            source_term.astype(jnp.bfloat16), "heads", scatter_dimension=0, tiled=True
        ).astype(jnp.float32),
        lax.psum_scatter(
            first_gain_part.astype(jnp.bfloat16), "heads", scatter_dimension=0, tiled=True
        ).astype(jnp.float32),
    )
    grad_tokens = (grad_resid + source_norm).astype(jnp.bfloat16)
    summed = (
        lax.psum_scatter(
            grad_query.astype(jnp.bfloat16), "fsdp", scatter_dimension=0, tiled=True
        ).astype(jnp.float32),
        lax.psum_scatter(
            grad_key.astype(jnp.bfloat16), "fsdp", scatter_dimension=0, tiled=True
        ).astype(jnp.float32),
        lax.psum_scatter(
            grad_value.astype(jnp.bfloat16), "fsdp", scatter_dimension=0, tiled=True
        ).astype(jnp.float32),
        lax.psum_scatter(
            grad_output.astype(jnp.bfloat16), "fsdp", scatter_dimension=1, tiled=True
        ).astype(jnp.float32),
        lax.psum_scatter(
            grad_hidden.astype(jnp.bfloat16), "fsdp", scatter_dimension=0, tiled=True
        ).astype(jnp.float32),
        lax.psum_scatter(
            grad_project.astype(jnp.bfloat16), "fsdp", scatter_dimension=1, tiled=True
        ).astype(jnp.float32),
        lax.psum_scatter(
            grad_hidden_bias.astype(jnp.bfloat16), "fsdp", scatter_dimension=0, tiled=True
        ).astype(jnp.float32),
        lax.psum_scatter(
            grad_output_bias.astype(jnp.bfloat16), "fsdp", scatter_dimension=0, tiled=True
        ).astype(jnp.float32),
        lax.psum_scatter(
            first_gain_cols.astype(jnp.bfloat16), "fsdp", scatter_dimension=0, tiled=True
        ).astype(jnp.float32),
        lax.psum_scatter(
            second_gain_cols.astype(jnp.bfloat16), "fsdp", scatter_dimension=0, tiled=True
        ).astype(jnp.float32),
    )
    return (
        mixed,
        grad_tokens,
        summed[0],
        summed[1],
        summed[2],
        summed[3],
        summed[4],
        summed[6],
        summed[5],
        summed[7],
        summed[8],
        summed[9],
    )


def solution(mesh):
    return jax.shard_map(
        local,
        mesh=mesh,
        in_specs=(
            P(("fsdp", "heads"), None),
            P("fsdp", "heads"),
            P("fsdp", "heads"),
            P("fsdp", "heads"),
            P("heads", "fsdp"),
            P("fsdp", "heads"),
            P(("heads", "fsdp")),
            P("heads", "fsdp"),
            P(("heads", "fsdp")),
            P(("heads", "fsdp")),
            P(("heads", "fsdp")),
            P("fsdp", None),
            P(("fsdp", "heads"), None),
        ),
        out_specs=(
            P(("fsdp", "heads"), None),
            P(("fsdp", "heads"), None),
            P("fsdp", "heads"),
            P("fsdp", "heads"),
            P("fsdp", "heads"),
            P("heads", "fsdp"),
            P("fsdp", "heads"),
            P(("heads", "fsdp")),
            P("heads", "fsdp"),
            P(("heads", "fsdp")),
            P(("heads", "fsdp")),
            P(("heads", "fsdp")),
        ),
        check_vma=False,
    )
```

profile of v0, /device:TPU:0, one launch (start us, length us, event | category | flops | bytes accessed | tf_op | source)
XLA Modules:
  0.0 1127.2 jit_solution(4536970500380907387)
XLA Ops:
  15.3 35.4 %all-reduce.12 = (bf16[640]{0:T(1024)(128)(2,1)S(1)}, bf16[640]{0:T(1024)(128)(2,1)S(1)}, bf16[640]{0:T(1024)(128)(2,1)S(1)}) all-reduce(bf16[640]{0:T(1024)(128)(2,1)S(1)} %dynamic-update-slice.1, bf16[640]{0:T(1024)(128)(2,1)S(1)} %dynamic-update-slice, ...), channel_id=1, replica_groups=mesh['fsdp'=16,'heads'=2] {'fsdp'}, use_global_device_ids=true, to_apply=%add.2 | all-reduce | flops 1920 | bytes 7680
  69.7 38.5 %all-gather.15.cloned.1.call-done = bf16[1280,640]{1,0:T(8,128)(2,1)} async-done(((bf16[80,640]{1,0:T(8,128)(2,1)}), bf16[1280,640]{1,0:T(8,128)(2,1)}) %all-gather.15.cloned.1.call-update) | async-done | bytes 1638416 | tf_op jit(solution)/shard_map/all_gather | solution.py:126
  108.2 5.9 convolution_convert_fusion.9
  123.0 26.1 %all-gather.17.cloned.1.call-done = bf16[1280,640]{1,0:T(8,128)(2,1)} async-done(((bf16[80,640]{1,0:T(8,128)(2,1)}), bf16[1280,640]{1,0:T(8,128)(2,1)}) %all-gather.17.cloned.1.call-update) | async-done | bytes 1638416 | tf_op jit(solution)/shard_map/all_gather | solution.py:124
  149.0 7.5 fusion.78
  156.5 8.1 reshape.159
  164.7 25.0 %all-gather.19.cloned.1.call-done = bf16[1280,640]{1,0:T(8,128)(2,1)} async-done(((bf16[80,640]{1,0:T(8,128)(2,1)}), bf16[1280,640]{1,0:T(8,128)(2,1)}) %all-gather.19.cloned.1.call-update) | async-done | bytes 1638416 | tf_op jit(solution)/shard_map/all_gather | solution.py:125
  189.7 7.6 fusion.76
  197.3 7.6 reshape.160
  204.9 5.5 subtract_convert_fusion.3
  210.4 7.9 pad_maximum_fusion
  222.1 25.4 %while.26 = (s32[]{:T(128)}, bf16[3,512,8,80]{1,3,2,0:T(8,128)(2,1)S(1)}, f32[3,8,512]{2,1,0:T(8,128)S(1)}, bf16[3,512,8,80]{1,3,2,0:T(8,128)(2,1)}, pred[3,512,...) while((s32[]{:T(128)}, ...), condition=%wide.region_8.9_spmd, body=%wide.region_5.8_spmd.sunk | while | flops 696578048 | bytes 29231204 | solution.py:174
  249.9 6.9 convolution_convert_fusion.1
  263.8 94.9 %all-reduce.16.cloned.1.call-done = bf16[1536,1280]{1,0:T(8,128)(2,1)} async-done(((bf16[1536,1280]{1,0:T(8,128)(2,1)}), bf16[1536,1280]{1,0:T(8,128)(2,1)}) %all-reduce.16.cloned.1.call-update) | async-done | bytes 3932176 | tf_op jit(solution)/shard_map/psum | solution.py:177
  358.7 4.7 multiply_reduce_fusion.3
  363.4 37.4 %all-gather.23.cloned.1.call-done = bf16[1280,640]{1,0:T(8,128)(2,1)} async-done(((bf16[80,640]{1,0:T(8,128)(2,1)}), bf16[1280,640]{1,0:T(8,128)(2,1)}) %all-gather.23.cloned.1.call-update) | async-done | bytes 1638416 | tf_op jit(solution)/shard_map/all_gather | solution.py:128
  400.8 9.4 fusion.72
  410.2 31.4 %all-gather.25.cloned.1.call-done = bf16[640,1280]{0,1:T(8,128)(2,1)} async-done(((bf16[640,80]{0,1:T(8,128)(2,1)}), bf16[640,1280]{0,1:T(8,128)(2,1)}) %all-gather.25.cloned.1.call-update) | async-done | bytes 1638416 | tf_op jit(solution)/shard_map/all_gather | solution.py:129
  441.6 54.1 %all-gather.27.cloned.1.call-done = bf16[1536,1280]{1,0:T(8,128)(2,1)} async-done(((bf16[768,1280]{1,0:T(8,128)(2,1)}), bf16[1536,1280]{1,0:T(8,128)(2,1)}) %all-gather.27.cloned.1.call-update) | async-done | bytes 3932176 | tf_op jit(solution)/shard_map/all_gather | solution.py:202
  495.7 9.8 fusion.81
  505.5 5.4 multiply_reduce_fusion.1
  510.9 5.5 subtract_convert_fusion
  516.5 52.2 %reduce-scatter.12.cloned.1.call-done = bf16[768,1280]{1,0:T(8,128)(2,1)} async-done(((bf16[1536,1280]{1,0:T(8,128)(2,1)}), bf16[768,1280]{1,0:T(8,128)(2,1)}) %reduce-scatter.12.cloned.1.call-update) | async-done | bytes 1966096 | tf_op jit(solution)/shard_map/reduce_scatter | solution.py:217
  572.0 8.0 convolution_convert_fusion.2
  580.1 9.5 convolution_convert_fusion.3
  589.9 8.5 convolution_convert_fusion
  598.5 27.4 %all-gather.29.cloned.1.call-done = bf16[1536,1280]{1,0:T(8,128)(2,1)} async-done(((bf16[768,1280]{1,0:T(8,128)(2,1)}), bf16[1536,1280]{1,0:T(8,128)(2,1)}) %all-gather.29.cloned.1.call-update) | async-done | bytes 3932176 | tf_op jit(solution)/shard_map/all_gather | solution.py:225
  625.9 6.6 convolution_convert_fusion.8
  632.5 6.5 reshape.193
  639.0 4.8 copy.100
  643.8 6.7 convolution_convert_fusion.4
  652.2 219.6 %while.27 = (s32[]{:T(128)}, f32[3,512,8,80]{1,0,3,2:T(4,128)}, f32[3,512,8,80]{1,0,3,2:T(4,128)}, bf16[3,512,8,80]{1,3,2,0:T(8,128)(2,1)}, bf16[3,512,8,80]{1,3...) while((s32[]{:T(128)}, f32[3,512,8,80]{1,0,3,2:T(4,128)}, ...), condition=%wide.region_16.17_spmd, body=%wide.region_14.16_spmd.sunk | while | flops 1710157824 | bytes 82693272 | solution.py:229
  673.2 26.0 %dynamic_update_slice.30 = f32[3,512,8,80]{1,0,3,2:T(4,128)} dynamic-update-slice(f32[3,512,8,80]{1,0,3,2:T(4,128)} %get-tuple-element.409, f32[1,512,8,80]{1,0,3,2:T(1,128)S(1)} %copy.137, s32[]{:T(128)S(6)} %copy.161, s32[]{:T(128)} %constant.76.clone.1..sunk, s32[]{:T(128)} %constant.76.clone.1..sunk, s32[]{:T(128)} %constant.76.clone.1..sunk) | dynamic-update-slice | bytes 2621444 | tf_op jit(solution)/shard_map/while/body/jit(dynamic_update_index_in_dim)/dynamic_update_slice | solution.py:229
  699.2 26.0 %dynamic_update_slice.29 = f32[3,512,8,80]{1,0,3,2:T(4,128)} dynamic-update-slice(f32[3,512,8,80]{1,0,3,2:T(4,128)} %get-tuple-element.408, f32[1,512,8,80]{1,0,3,2:T(1,128)S(1)} %copy.136, s32[]{:T(128)S(6)} %copy.161, s32[]{:T(128)} %constant.76.clone.1..sunk, s32[]{:T(128)} %constant.76.clone.1..sunk, s32[]{:T(128)} %constant.76.clone.1..sunk) | dynamic-update-slice | bytes 2621444 | tf_op jit(solution)/shard_map/while/body/jit(dynamic_update_index_in_dim)/dynamic_update_slice | solution.py:229
  746.2 26.1 %dynamic_update_slice.30 = f32[3,512,8,80]{1,0,3,2:T(4,128)} dynamic-update-slice(f32[3,512,8,80]{1,0,3,2:T(4,128)} %get-tuple-element.409, f32[1,512,8,80]{1,0,3,2:T(1,128)S(1)} %copy.137, s32[]{:T(128)S(6)} %copy.161, s32[]{:T(128)} %constant.76.clone.1..sunk, s32[]{:T(128)} %constant.76.clone.1..sunk, s32[]{:T(128)} %constant.76.clone.1..sunk) | dynamic-update-slice | bytes 2621444 | tf_op jit(solution)/shard_map/while/body/jit(dynamic_update_index_in_dim)/dynamic_update_slice | solution.py:229
  772.3 26.0 %dynamic_update_slice.29 = f32[3,512,8,80]{1,0,3,2:T(4,128)} dynamic-update-slice(f32[3,512,8,80]{1,0,3,2:T(4,128)} %get-tuple-element.408, f32[1,512,8,80]{1,0,3,2:T(1,128)S(1)} %copy.136, s32[]{:T(128)S(6)} %copy.161, s32[]{:T(128)} %constant.76.clone.1..sunk, s32[]{:T(128)} %constant.76.clone.1..sunk, s32[]{:T(128)} %constant.76.clone.1..sunk) | dynamic-update-slice | bytes 2621444 | tf_op jit(solution)/shard_map/while/body/jit(dynamic_update_index_in_dim)/dynamic_update_slice | solution.py:229
  819.3 26.0 %dynamic_update_slice.30 = f32[3,512,8,80]{1,0,3,2:T(4,128)} dynamic-update-slice(f32[3,512,8,80]{1,0,3,2:T(4,128)} %get-tuple-element.409, f32[1,512,8,80]{1,0,3,2:T(1,128)S(1)} %copy.137, s32[]{:T(128)S(6)} %copy.161, s32[]{:T(128)} %constant.76.clone.1..sunk, s32[]{:T(128)} %constant.76.clone.1..sunk, s32[]{:T(128)} %constant.76.clone.1..sunk) | dynamic-update-slice | bytes 2621444 | tf_op jit(solution)/shard_map/while/body/jit(dynamic_update_index_in_dim)/dynamic_update_slice | solution.py:229
  845.4 26.0 %dynamic_update_slice.29 = f32[3,512,8,80]{1,0,3,2:T(4,128)} dynamic-update-slice(f32[3,512,8,80]{1,0,3,2:T(4,128)} %get-tuple-element.408, f32[1,512,8,80]{1,0,3,2:T(1,128)S(1)} %copy.136, s32[]{:T(128)S(6)} %copy.161, s32[]{:T(128)} %constant.76.clone.1..sunk, s32[]{:T(128)} %constant.76.clone.1..sunk, s32[]{:T(128)} %constant.76.clone.1..sunk) | dynamic-update-slice | bytes 2621444 | tf_op jit(solution)/shard_map/while/body/jit(dynamic_update_index_in_dim)/dynamic_update_slice | solution.py:229
  877.2 5.2 convolution_convert_fusion.5
  882.5 6.3 add_convert_fusion.2
  891.2 5.1 convolution_convert_fusion.6
  901.6 5.2 convolution_convert_fusion.7
  907.0 5.6 fusion.84
  916.0 6.4 fusion.63
  933.7 5.0 all-reduce.13
  938.9 60.2 %all-reduce.11 = (bf16[640]{0:T(1024)(128)(2,1)S(1)}, bf16[640]{0:T(1024)(128)(2,1)S(1)}, bf16[640]{0:T(1024)(128)(2,1)S(1)}, bf16[640]{0:T(1024)(128)(2,1)S(1)}, bf16[640]{0:T(1024)(128)(2,1)S(1)}) all-reduce(bf16[640]{0:T(1024)(128)(2,1)S(1)} %dynamic-update-slice.3, ...), channel_id=1, replica_groups=mesh['fsdp'=16,'heads'=2] {'fsdp'}, use_global_device_ids=true, to_apply=%add.4 | all-reduce | flops 3200 | bytes 12800
  1015.2 47.8 %reduce-scatter.16.cloned.1.call-done = bf16[80,640]{1,0:T(8,128)(2,1)} async-done(((bf16[1280,640]{1,0:T(8,128)(2,1)}), bf16[80,640]{1,0:T(8,128)(2,1)}) %reduce-scatter.16.cloned.1.call-update) | async-done | bytes 102416 | tf_op jit(solution)/shard_map/reduce_scatter | solution.py:255
  1064.5 51.8 %reduce-scatter.14.cloned.1.call-done = bf16[768,1280]{1,0:T(8,128)(2,1)} async-done(((bf16[1536,1280]{1,0:T(8,128)(2,1)}), bf16[768,1280]{1,0:T(8,128)(2,1)}) %reduce-scatter.14.cloned.1.call-update) | async-done | bytes 1966096 | tf_op jit(solution)/shard_map/reduce_scatter | solution.py:246
  (232 shorter events, 190.1 us)
Async XLA Ops:
  7.2 58.9 %all-gather.13.cloned.1.call-start = ((), (), s32[]{:S(2)}) async-start(), calls=%async_computation.9 | async-start | bytes 5898240 | tf_op jit(solution)/shard_map/all_gather | solution.py:148
  7.9 100.3 %all-gather.15.cloned.1.call-start = ((), (), s32[]{:S(2)}) async-start(), calls=%async_computation.10 | async-start | bytes 1740800 | tf_op jit(solution)/shard_map/all_gather | solution.py:126
  8.7 140.4 %all-gather.17.cloned.1.call-start = ((), (), s32[]{:S(2)}) async-start(), calls=%async_computation.11 | async-start | bytes 1740800 | tf_op jit(solution)/shard_map/all_gather | solution.py:124
  9.4 180.3 %all-gather.19.cloned.1.call-start = ((), (), s32[]{:S(2)}) async-start(), calls=%async_computation.12 | async-start | bytes 1740800 | tf_op jit(solution)/shard_map/all_gather | solution.py:125
  10.0 240.0 %all-gather.21.cloned.1.call-start = ((), (), s32[]{:S(2)}) async-start(), calls=%async_computation.13 | async-start | bytes 1740800 | tf_op jit(solution)/shard_map/all_gather | solution.py:127
  10.6 348.1 %all-reduce.16.cloned.1.call-start = ((), (), s32[]{:S(2)}) async-start(), calls=%async_computation.14 | async-start | bytes 7864320 | tf_op jit(solution)/shard_map/psum | solution.py:177
  55.3 134.4 %copy-start.21 = (f32[1280]{0:T(1024)}, f32[1280]{0:T(1024)S(1)}, u32[]{:S(2)}) copy-start(f32[1280]{0:T(1024)S(1)} %reshape.182) | copy-start | bytes 15364
  61.6 143.4 %copy-start.8 = (f32[3,512,40]{1,0,2:T(4,128)}, f32[3,512,40]{1,0,2:T(4,128)S(1)}, u32[]{:S(2)}) copy-start(f32[3,512,40]{1,0,2:T(4,128)S(1)} %get-tuple-element.247) | copy-start | bytes 737284
  61.6 143.4 %copy-start.10 = (f32[3,512,40]{1,0,2:T(4,128)}, f32[3,512,40]{1,0,2:T(4,128)S(1)}, u32[]{:S(2)}) copy-start(f32[3,512,40]{1,0,2:T(4,128)S(1)} %get-tuple-element.248) | copy-start | bytes 737284
  69.7 120.0 %copy-start.19 = (f32[1536]{0:T(1024)}, f32[1536]{0:T(1024)S(1)}, u32[]{:S(2)}) copy-start(f32[1536]{0:T(1024)S(1)} %get-tuple-element.250) | copy-start | bytes 18436
  249.9 6.9 copy-start.12
  256.9 143.9 %all-gather.23.cloned.1.call-start = ((), (), s32[]{:S(2)}) async-start(), calls=%async_computation.15 | async-start | bytes 1740800 | tf_op jit(solution)/shard_map/all_gather | solution.py:128
  257.6 184.0 %all-gather.25.cloned.1.call-start = ((), (), s32[]{:S(2)}) async-start(), calls=%async_computation.16 | async-start | bytes 1740800 | tf_op jit(solution)/shard_map/all_gather | solution.py:129
  258.4 237.3 %all-gather.27.cloned.1.call-start = ((), (), s32[]{:S(2)}) async-start(), calls=%async_computation.18 | async-start | bytes 5898240 | tf_op jit(solution)/shard_map/all_gather | solution.py:202
  259.1 309.6 %reduce-scatter.12.cloned.1.call-start = ((), (), s32[]{:S(2)}) async-start(), calls=%async_computation.19 | async-start | bytes 5898240 | tf_op jit(solution)/shard_map/reduce_scatter | solution.py:217
  410.2 95.3 %copy-start.27 = (bf16[1280,640]{1,0:T(8,128)(2,1)S(1)}, bf16[1280,640]{1,0:T(8,128)(2,1)}, u32[]{:S(2)}) copy-start(bf16[1280,640]{1,0:T(8,128)(2,1)} %all-gather.23.cloned.1.call-done) | copy-start | bytes 4915204
  495.7 9.8 copy-start
  495.7 9.8 copy-start.7
  505.5 5.4 copy-start.30
  516.4 52.3 %copy-start.5 = (bf16[768,1280]{1,0:T(8,128)(2,1)S(1)}, bf16[768,1280]{1,0:T(8,128)(2,1)}, u32[]{:S(2)}) copy-start(bf16[768,1280]{1,0:T(8,128)(2,1)} %param.29) | copy-start | bytes 5898244
  516.4 109.4 %all-gather.29.cloned.1.call-start = ((), (), s32[]{:S(2)}) async-start(), calls=%async_computation.20 | async-start | bytes 5898240 | tf_op jit(solution)/shard_map/all_gather | solution.py:225
  572.0 358.6 %reduce-scatter.26.cloned.1.call-start = ((), (), s32[]{:S(2)}) async-start(), calls=%async_computation.27 | async-start | bytes 1740800 | tf_op jit(solution)/shard_map/reduce_scatter | solution.py:270
  580.0 9.8 copy-start.26
  580.1 352.1 %reduce-scatter.24.cloned.1.call-start = ((), (), s32[]{:S(2)}) async-start(), calls=%async_computation.26 | async-start | bytes 1740800 | tf_op jit(solution)/shard_map/reduce_scatter | solution.py:267
  589.6 416.2 %reduce-scatter.10.cloned.1.call-start = ((), (), s32[]{:S(2)}) async-start(), calls=%async_computation.17 | async-start | bytes 5898240 | tf_op jit(solution)/shard_map/reduce_scatter | solution.py:187
  598.4 27.5 %copy-start.25 = (bf16[640,1280]{0,1:T(8,128)(2,1)S(1)}, bf16[640,1280]{0,1:T(8,128)(2,1)}, u32[]{:S(2)}) copy-start(bf16[640,1280]{0,1:T(8,128)(2,1)} %all-gather.21.cloned.1.call-done) | copy-start | bytes 4915204
  598.4 412.0 %reduce-scatter.22.cloned.1.call-start = ((), (), s32[]{:S(2)}) async-start(), calls=%async_computation.25 | async-start | bytes 1740800 | tf_op jit(solution)/shard_map/reduce_scatter | solution.py:264
  632.5 11.3 %copy-start.13 = (bf16[80,8,3,512]{3,1,2,0:T(8,128)(2,1)S(1)}, bf16[80,8,3,512]{3,1,2,0:T(8,128)(2,1)}, u32[]{:S(2)}) copy-start(bf16[80,8,3,512]{3,1,2,0:T(8,128)(2,1)} %copy-done.12) | copy-start | bytes 5898244
  650.5 361.5 %reduce-scatter.20.cloned.1.call-start = ((), (), s32[]{:S(2)}) async-start(), calls=%async_computation.24 | async-start | bytes 1740800 | tf_op jit(solution)/shard_map/reduce_scatter | solution.py:261
  871.8 5.4 copy-start.1
  871.8 5.4 copy-start.20
  871.8 5.4 copy-start.22
  875.9 1.3 copy-start.14
  877.2 5.3 copy-start.9
  877.2 5.3 copy-start.11
  882.5 131.1 %reduce-scatter.18.cloned.1.call-start = ((), (), s32[]{:S(2)}) async-start(), calls=%async_computation.23 | async-start | bytes 1740800 | tf_op jit(solution)/shard_map/reduce_scatter | solution.py:258
  888.8 2.4 copy-start.2
  896.3 166.6 %reduce-scatter.16.cloned.1.call-start = ((), (), s32[]{:S(2)}) async-start(), calls=%async_computation.22 | async-start | bytes 1740800 | tf_op jit(solution)/shard_map/reduce_scatter | solution.py:255
  896.4 5.2 copy-start.3
  906.7 209.6 %reduce-scatter.14.cloned.1.call-start = ((), (), s32[]{:S(2)}) async-start(), calls=%async_computation.21 | async-start | bytes 5898240 | tf_op jit(solution)/shard_map/reduce_scatter | solution.py:246
  907.0 5.7 copy-start.17
  912.6 3.3 copy-start.4
  912.6 3.3 copy-start.15
  916.0 6.4 copy-start.18
  925.8 2.6 copy-start.28
  925.8 7.9 copy-start.23
  925.8 13.1 %copy-start.24 = (bf16[640]{0:T(1024)(128)(2,1)S(1)}, bf16[640]{0:T(1024)(128)(2,1)}, u32[]{:S(2)}) copy-start(bf16[640]{0:T(1024)(128)(2,1)} %get-tuple-element.227) | copy-start | bytes 3844
  1005.8 110.5 %copy-start.6 = (bf16[768,1280]{1,0:T(8,128)(2,1)S(1)}, bf16[768,1280]{1,0:T(8,128)(2,1)}, u32[]{:S(2)}) copy-start(bf16[768,1280]{1,0:T(8,128)(2,1)} %param.29) | copy-start | bytes 5898244
  (2 other events, 1.9 us)
Sparse Core Ops, SparseCore 0:
  9.5 56.5 all-gather.12
  68.3 39.8 all-gather.14
  110.4 38.5 all-gather.16
  151.1 38.5 all-gather.18
  191.7 38.6 all-gather.20
  257.0 101.6 all-reduce.15
  360.9 39.8 all-gather.22
  403.0 38.5 all-gather.24
  443.2 52.4 all-gather.26
  516.6 52.0 reduce-scatter.11
  572.1 53.7 all-gather.28
  629.5 58.2 reduce-scatter.25
  691.5 57.2 reduce-scatter.23
  751.0 51.1 reduce-scatter.9
  805.7 58.2 reduce-scatter.21
  882.6 58.2 reduce-scatter.19
  944.5 57.4 reduce-scatter.17
  1005.6 57.2 reduce-scatter.15
  1065.2 51.0 reduce-scatter.13
where the time goes:
time: 1140 us; the launch traced here: 1130 us
  waiting for transfers between devices  496 us (44%)
  local copies, waits for them, and re-layouts  222 us (19%)
  matrix products  189 us (17%)
  blocking collectives  114 us (10%)
  other arithmetic  86.1 us (8%)
  between operations  16.7 us (1%)
    dynamic_update_slice x12, local copies, waits for them, and re-layouts, local(): lax.map(attend_back_row, (queries, keys, values, allowed, logsum, grad_he...  164 us
    unnamed x3, blocking collectives  101 us
    psum x1, waiting for transfers between devices, local(): lax.psum(branch.astype(jnp.bfloat16), 'heads').astype(jnp.float32)  94.9 us
    all_gather x1, waiting for transfers between devices, local(): grad_whole = lax.all_gather(cotangent, 'heads', axis=0, tiled=True)  54.1 us
    reduce_scatter x1, waiting for transfers between devices, local(): lax.psum_scatter(resid_term.astype(jnp.bfloat16), 'heads', scatter_dimens...  52.2 us
    reduce_scatter x1, waiting for transfers between devices, local(): lax.psum_scatter(source_term.astype(jnp.bfloat16), 'heads', scatter_dimen...  51.8 us
    reduce_scatter x1, waiting for transfers between devices, local(): lax.psum_scatter(grad_query.astype(jnp.bfloat16), 'fsdp', scatter_dimensi...  47.8 us
    dot_general x6, matrix products, contract_first(): lax.dot_general(left, right, (((0,), (0,)), ((), ())), preferred_element_...  39.7 us
  transfers between devices with their start and end apart: 19, of which 12 were waited for; matrix products, arithmetic and copies ran while one was open for 41% of the time, Pallas kernels for 0%

commit v1 on v0

v1 whole, which is shorter than its diff:
```python
from functools import partial
import math

import jax
import jax.numpy as jnp
from jax import lax
from jax.experimental import pallas as pl
from jax.experimental.pallas import tpu as pltpu
from jax.sharding import PartitionSpec as P

HEAD_DIM = 80
ROW = 512
MOST = 64
EPS = 1e-06
NEG = -1e30
THETA = 10000.0
ALL = ("fsdp", "heads")
BF = jnp.bfloat16
F32 = jnp.float32
VMEM_LIMIT = 60 * 1024 * 1024


def bits_of(n):
    return n.bit_length() - 1


def reverse_bits(values, count):
    out = 0
    for bit in range(count):
        out = out | (((values >> bit) & 1) << (count - 1 - bit))
    return out


class Links:
    def __init__(self, fsdp, heads):
        self.count = fsdp * heads
        self.hbits, self.fbits = bits_of(heads), bits_of(fsdp)
        desc = list(range(self.hbits + self.fbits - 1, self.hbits - 1, -1))
        self.z, self.x, self.core = desc[:-2], desc[-2:-1], desc[-1:]
        self.y = list(range(self.hbits - 1, -1, -1))

    def swap(self, value, bit):
        pairs = [(d, d ^ (1 << bit)) for d in range(self.count)]
        return lax.ppermute(value, ALL, pairs)

    def join(self, value, bit, axis):
        return jnp.concatenate([value, self.swap(value, bit)], axis=axis)

    def order(self, first):
        x = [(b, 0) for b in self.x]
        y = [(b, 1) for b in self.y]
        return x + y if first == "x" else y + x

    def gather_pair(self, left, right):
        both = jnp.stack([left, right])
        for bit in self.z:
            both = self.join(both, bit, 1)
        out = []
        for value, first in ((both[0], "x"), (both[1], "y")):
            for bit, axis in self.order(first):
                value = self.join(value, bit, axis)
            for bit in self.core:
                value = self.join(value, bit, 0)
            out.append(value)
        return out

    def fold(self, value, bit, axis):
        half = value.shape[axis] // 2
        keep = lax.slice_in_dim(value, 0, half, axis=axis)
        send = lax.slice_in_dim(value, half, 2 * half, axis=axis)
        return keep + self.swap(send.astype(BF), bit).astype(F32)

    def scatter_pair(self, left, right):
        out = []
        for value, first in ((left, "y"), (right, "x")):
            for bit in self.core:
                value = self.fold(value, bit, 0)
            other = "x" if first == "y" else "y"
            for bit, axis in reversed(self.order(other)):
                value = self.fold(value, bit, axis)
            out.append(value)
        both = jnp.stack(out)
        for bit in reversed(self.z):
            both = self.fold(both, bit, 1)
        return both[0], both[1]


def flip_kernel(parts, source, x_ref, out_ref, held):
    size = x_ref.shape[1] // parts
    held[...] = x_ref[...].astype(F32).T
    for part in range(parts):
        start = pl.multiple_of(source[part] * size, 8)
        out_ref[part * size : (part + 1) * size, :] = held[pl.ds(start, size), :]


def flip(value, source, parts):
    rows, cols = value.shape
    return pl.pallas_call(
        partial(flip_kernel, parts),
        out_shape=jax.ShapeDtypeStruct((cols, rows), F32),
        in_specs=[
            pl.BlockSpec(memory_space=pltpu.SMEM),
            pl.BlockSpec(memory_space=pltpu.VMEM),
        ],
        out_specs=pl.BlockSpec(memory_space=pltpu.VMEM),
        scratch_shapes=[pltpu.VMEM((cols, rows), F32)],
        compiler_params=pltpu.CompilerParams(vmem_limit_bytes=VMEM_LIMIT),
    )(source, value)


def unflip_kernel(parts, source, x_ref, out_ref, held):
    size = x_ref.shape[0] // parts
    for part in range(parts):
        start = pl.multiple_of(source[part] * size, 8)
        held[pl.ds(start, size), :] = x_ref[part * size : (part + 1) * size, :]
    out_ref[...] = held[...].T.astype(BF)


def unflip(value, source, parts):
    rows, cols = value.shape
    return pl.pallas_call(
        partial(unflip_kernel, parts),
        out_shape=jax.ShapeDtypeStruct((cols, rows), BF),
        in_specs=[
            pl.BlockSpec(memory_space=pltpu.SMEM),
            pl.BlockSpec(memory_space=pltpu.VMEM),
        ],
        out_specs=pl.BlockSpec(memory_space=pltpu.VMEM),
        scratch_shapes=[pltpu.VMEM((rows, cols), F32)],
        compiler_params=pltpu.CompilerParams(vmem_limit_bytes=VMEM_LIMIT),
    )(source, value)


def turn(vectors, cosine, sine):
    half = vectors.shape[0] // 2
    first, second = vectors[:half], vectors[half:]
    return jnp.concatenate([first * cosine - second * sine, second * cosine + first * sine], axis=0)


def dot_tn(left, right):
    return lax.dot_general(left, right, (((0,), (0,)), ((), ())), preferred_element_type=F32)


def dot_nn(left, right):
    return lax.dot_general(left, right, (((1,), (0,)), ((), ())), preferred_element_type=F32)


def dot_nt(left, right):
    return lax.dot_general(left, right, (((1,), (1,)), ((), ())), preferred_element_type=F32)


def fill_bias(begin_ref, bias_ref, halo, block, window):
    blocks = bias_ref.shape[0]
    for b in range(blocks):
        low = b * block
        key = lax.broadcasted_iota(jnp.int32, (window, block), 0) + low
        query = lax.broadcasted_iota(jnp.int32, (window, block), 1) + (halo + low)
        begin = begin_ref[0:1, low : low + block]
        bias_ref[b] = jnp.where((key >= begin) & (key <= query), 0.0, NEG)


def attend_kernel(halo, block, q_ref, k_ref, v_ref, cos_ref, sin_ref, begin_ref,
                  qr_ref, kr_ref, vr_ref, att_ref, log_ref, bias_ref):
    own = q_ref.shape[1]
    window = halo + block
    scale = HEAD_DIM ** (-0.5)

    @pl.when(pl.program_id(0) == 0)
    def _():
        fill_bias(begin_ref, bias_ref, halo, block, window)

    cosine, sine = cos_ref[...], sin_ref[...]
    q = turn(q_ref[...], cosine[:, halo:], sine[:, halo:]).astype(BF)
    k = turn(k_ref[...], cosine, sine).astype(BF)
    v = v_ref[...].astype(BF)
    qr_ref[...] = q
    kr_ref[...] = k
    vr_ref[...] = v
    for b in range(own // block):
        low = b * block
        qb, kb, vb = q[:, low : low + block], k[:, low : low + window], v[:, low : low + window]
        scores = dot_tn(kb, qb) * scale + bias_ref[b]
        peak = jnp.max(scores, axis=0, keepdims=True)
        expo = jnp.exp(scores - peak)
        total = jnp.sum(expo, axis=0, keepdims=True)
        weights = (expo / total).astype(BF)
        att_ref[:, low : low + block] = dot_nn(vb, weights).astype(BF)
        log_ref[0, :, low : low + block] = peak + jnp.log(total)


def attend(q, k, v, cosine, sine, begin, halo, block):
    inner, own = q.shape
    total = halo + own
    heads = inner // HEAD_DIM
    per = lambda n: pl.BlockSpec((HEAD_DIM, n), lambda i: (i, 0))
    full = lambda a: pl.BlockSpec(a.shape, lambda i: (0, 0))
    return pl.pallas_call(
        partial(attend_kernel, halo, block),
        grid=(heads,),
        out_shape=(
            jax.ShapeDtypeStruct((inner, own), BF),
            jax.ShapeDtypeStruct((inner, total), BF),
            jax.ShapeDtypeStruct((inner, total), BF),
            jax.ShapeDtypeStruct((inner, own), BF),
            jax.ShapeDtypeStruct((heads, 1, own), F32),
        ),
        in_specs=[per(own), per(total), per(total), full(cosine), full(sine), full(begin)],
        out_specs=(per(own), per(total), per(total), per(own), pl.BlockSpec((1, 1, own), lambda i: (i, 0, 0))),
        scratch_shapes=[pltpu.VMEM((own // block, halo + block, block), F32)],
        compiler_params=pltpu.CompilerParams(vmem_limit_bytes=VMEM_LIMIT),
    )(q, k, v, cosine, sine, begin)


def attend_back_kernel(halo, block, q_ref, k_ref, v_ref, g_ref, log_ref, cos_ref, sin_ref, begin_ref,
                       dq_ref, dk_ref, dv_ref, dkh_ref, dvh_ref, bias_ref, dk_sum, dv_sum):
    own = q_ref.shape[1]
    window = halo + block
    scale = HEAD_DIM ** (-0.5)

    @pl.when(pl.program_id(0) == 0)
    def _():
        fill_bias(begin_ref, bias_ref, halo, block, window)

    cosine, sine = cos_ref[...], sin_ref[...]
    dk_sum[...] = jnp.zeros_like(dk_sum)
    dv_sum[...] = jnp.zeros_like(dv_sum)
    for b in range(own // block):
        low = b * block
        mine, seen = slice(low, low + block), slice(low, low + window)
        qb, kb, vb, gb = q_ref[:, mine], k_ref[:, seen], v_ref[:, seen], g_ref[:, mine]
        scores = dot_tn(kb, qb) * scale + bias_ref[b]
        probs = jnp.exp(scores - log_ref[0, :, mine])
        dv_sum[:, seen] += dot_nt(gb, probs.astype(BF))
        grad_probs = dot_tn(vb, gb)
        inner = jnp.sum(probs * grad_probs, axis=0, keepdims=True)
        grad_scores = (probs * (grad_probs - inner)).astype(BF)
        dq = dot_nn(kb, grad_scores) * scale
        dk_sum[:, seen] += dot_nt(qb, grad_scores)
        own_seen = slice(halo + low, halo + low + block)
        dq_ref[:, mine] = turn(dq, cosine[:, own_seen], -sine[:, own_seen]).astype(BF)
    dk = turn(dk_sum[...] * scale, cosine, -sine).astype(BF)
    dk_ref[...] = dk[:, halo:]
    dkh_ref[...] = dk[:, :halo]
    dv = dv_sum[...].astype(BF)
    dv_ref[...] = dv[:, halo:]
    dvh_ref[...] = dv[:, :halo]


def attend_back(q, k, v, g, logs, cosine, sine, begin, halo, block):
    inner, own = q.shape
    total = halo + own
    heads = inner // HEAD_DIM
    per = lambda n: pl.BlockSpec((HEAD_DIM, n), lambda i: (i, 0))
    full = lambda a: pl.BlockSpec(a.shape, lambda i: (0, 0))
    return pl.pallas_call(
        partial(attend_back_kernel, halo, block),
        grid=(heads,),
        out_shape=tuple(jax.ShapeDtypeStruct((inner, n), BF) for n in (own, own, own, halo, halo)),
        in_specs=[per(own), per(total), per(total), per(own), pl.BlockSpec((1, 1, own), lambda i: (i, 0, 0)),
                  full(cosine), full(sine), full(begin)],
        out_specs=tuple(per(n) for n in (own, own, own, halo, halo)),
        scratch_shapes=[
            pltpu.VMEM((own // block, halo + block, block), F32),
            pltpu.VMEM((HEAD_DIM, total), F32),
            pltpu.VMEM((HEAD_DIM, total), F32),
        ],
        compiler_params=pltpu.CompilerParams(vmem_limit_bytes=VMEM_LIMIT),
    )(q, k, v, g, logs, cosine, sine, begin)


def norm_back(grad_norm, source, factor, gain):
    scaled = gain * grad_norm
    inner = jnp.mean(scaled * source, axis=0, keepdims=True)
    grad_source = factor * scaled - source * (factor * factor * factor) * inner
    return grad_source, jnp.sum(grad_norm * source * factor, axis=1)


def local(fsdp, heads, tokens, w_query, w_key, w_value, w_output, w_hidden, bias_hidden, w_project,
          bias_output, gain_first, gain_second, lengths, cotangent):
    links = Links(fsdp, heads)
    own, width = tokens.shape
    inner = w_query.shape[1] * heads
    f_at, h_at = lax.axis_index("fsdp"), lax.axis_index("heads")
    me = f_at * heads + h_at
    halo = 128 if own % 128 == 0 else MOST
    block = 256 if own % 256 == 0 else own
    source = f_at ^ reverse_bits(jnp.arange(fsdp, dtype=jnp.int32), links.fbits)
    back = reverse_bits(jnp.arange(fsdp, dtype=jnp.int32) ^ f_at, links.fbits)
    inner_source = h_at ^ reverse_bits(jnp.arange(heads, dtype=jnp.int32), links.hbits)
    inner_back = reverse_bits(jnp.arange(heads, dtype=jnp.int32) ^ h_at, links.hbits)

    small = jnp.concatenate([bias_hidden, bias_output, gain_first, gain_second])[None]
    piece = bias_hidden.shape[0]
    for bit in range(links.hbits + links.fbits):
        small = links.join(small, bit, 0)
    small = small[me ^ jnp.arange(fsdp * heads, dtype=jnp.int32)].astype(F32)
    small = small.reshape(fsdp, heads, 4, piece).transpose(2, 1, 0, 3).reshape(4, -1)

    def to_rel(vector):
        return vector.reshape(fsdp, -1)[source].reshape(-1, 1)

    shift_hidden = small[0].reshape(heads, -1)[inner_source].reshape(-1, 1)
    shift_output, gain_one, gain_two = to_rel(small[1]), to_rel(small[2]), to_rel(small[3])

    before = lax.ppermute(tokens[own - MOST :], "heads", [(i, i + 1) for i in range(heads - 1)])
    seen = jnp.concatenate([jnp.zeros((halo - MOST, width), tokens.dtype), before, tokens], axis=0)

    ends = jnp.cumsum(lengths, axis=1, dtype=jnp.int32)
    place = jnp.arange(ROW, dtype=jnp.int32)
    done = ends[:, None, :] <= place[None, :, None]
    offset = jnp.sum(jnp.where(done, lengths[:, None, :], 0), axis=2, dtype=jnp.int32)
    spot = (place[None] - offset).reshape(-1)
    spot = jnp.concatenate([jnp.zeros((halo,), jnp.int32), spot])
    spot = lax.dynamic_slice_in_dim(spot, h_at * own, halo + own, 0)
    begin = (jnp.arange(own, dtype=jnp.int32) + halo - spot[halo:])[None]
    half = HEAD_DIM // 2
    freq = jnp.exp(-jnp.arange(half, dtype=F32) * (2.0 * math.log(THETA) / HEAD_DIM))
    angle = freq[:, None] * spot.astype(F32)[None]
    cosine, sine = jnp.cos(angle), jnp.sin(angle)

    full_query, full_key = links.gather_pair(w_query, w_key)
    full_value, full_output = links.gather_pair(w_value, w_output.T)
    full_hidden, full_project = links.gather_pair(w_hidden, w_project.T)

    x = flip(seen, source, fsdp)
    cot = flip(cotangent, source, fsdp)
    factor_one = lax.rsqrt(jnp.mean(x * x, axis=0, keepdims=True) + EPS)
    normed = (x * factor_one * gain_one).astype(BF)
    normed_own = normed[:, halo:]
    source_own = x[:, halo:]
    factor_own = factor_one[:, halo:]

    q = dot_tn(full_query, normed_own)
    k = dot_tn(full_key, normed)
    v = dot_tn(full_value, normed)
    q, k, v, attended, logs = attend(q, k, v, cosine, sine, begin, halo, block)
    resid = source_own + dot_nn(full_output, attended)
    factor_two = lax.rsqrt(jnp.mean(resid * resid, axis=0, keepdims=True) + EPS)
    second = (resid * factor_two * gain_two).astype(BF)
    hidden = dot_tn(full_hidden, second) + shift_hidden
    active_full, pull = jax.vjp(partial(jax.nn.gelu, approximate=True), hidden)
    active = active_full.astype(BF)
    cot_low = cot.astype(BF)
    grad_project = dot_nt(cot_low, active)
    mixed = resid + dot_nn(full_project, active) + shift_output

    grad_output_bias = jnp.sum(cot, axis=1)
    grad_pre = pull(dot_tn(full_project, cot_low))[0].astype(BF)
    grad_hidden_bias = jnp.sum(grad_pre.astype(F32), axis=1)
    grad_hidden = dot_nt(second, grad_pre)
    grad_second = dot_nn(full_hidden, grad_pre)
    resid_term, grad_gain_second = norm_back(grad_second, resid, factor_two, gain_two)
    grad_resid = cot + resid_term
    grad_branch = grad_resid.astype(BF)
    grad_output = dot_nt(grad_branch, attended)
    grad_attended = dot_tn(full_output, grad_branch).astype(BF)
    dq, dk, dv, dk_halo, dv_halo = attend_back(q, k, v, grad_attended, logs, cosine, sine, begin, halo, block)
    extra = jnp.concatenate([dk_halo[:, halo - MOST :], dv_halo[:, halo - MOST :]], axis=0)
    extra = lax.ppermute(extra, "heads", [(i + 1, i) for i in range(heads - 1)]).astype(F32)
    shuffle = reverse_bits((h_at + 1) ^ h_at, links.hbits) ^ jnp.arange(heads, dtype=jnp.int32)
    groups = extra.reshape(2, heads, -1, MOST)
    extra = (groups[:, ::-1] if heads == 2 else groups[:, shuffle]).reshape(extra.shape)
    tail = jnp.pad(extra, ((0, 0), (own - MOST, 0)))
    dk = (dk.astype(F32) + tail[:inner]).astype(BF)
    dv = (dv.astype(F32) + tail[inner:]).astype(BF)
    grad_query = dot_nt(normed_own, dq)
    grad_key = dot_nt(normed_own, dk)
    grad_value = dot_nt(normed_own, dv)
    grad_normed = dot_nn(full_query, dq) + dot_nn(full_key, dk) + dot_nn(full_value, dv)
    source_term, grad_gain_first = norm_back(grad_normed, source_own, factor_own, gain_one)
    grad_tokens = grad_resid + source_term

    out_project, out_hidden = links.scatter_pair(grad_project, grad_hidden)
    out_output, out_value = links.scatter_pair(grad_output, grad_value)
    out_query, out_key = links.scatter_pair(grad_query, grad_key)

    def to_abs(vector):
        return vector.reshape(fsdp, -1)[back].reshape(-1)

    vecs = jnp.stack([
        grad_hidden_bias.reshape(heads, -1)[inner_back].reshape(-1),
        to_abs(grad_output_bias), to_abs(grad_gain_first), to_abs(grad_gain_second),
    ])
    vecs = vecs.reshape(4, heads, fsdp, piece).transpose(2, 1, 0, 3).reshape(fsdp * heads, 4 * piece)
    vecs = vecs[me ^ jnp.arange(fsdp * heads, dtype=jnp.int32)]
    for bit in reversed(range(links.hbits + links.fbits)):
        rows = vecs.shape[0] // 2
        vecs = vecs[:rows] + links.swap(vecs[rows:], bit)
    vecs = vecs.reshape(4, piece)

    return (
        unflip(mixed, source, fsdp),
        unflip(grad_tokens, source, fsdp),
        out_query, out_key, out_value, out_output.T, out_hidden,
        vecs[0], out_project.T, vecs[1], vecs[2], vecs[3],
    )


def solution(mesh):
    fsdp, heads = mesh.shape["fsdp"], mesh.shape["heads"]
    rows, cols = P("fsdp", "heads"), P("heads", "fsdp")
    tokens, vector = P(("fsdp", "heads"), None), P(("heads", "fsdp"))
    return jax.shard_map(
        partial(local, fsdp, heads),
        mesh=mesh,
        in_specs=(tokens, rows, rows, rows, cols, rows, vector, cols, vector, vector, vector, P("fsdp", None), tokens),
        out_specs=(tokens, tokens, rows, rows, rows, cols, rows, vector, cols, vector, vector, vector),
        check_vma=False,
    )
```

time: 1140 us -> 558 us (0.49)
  waiting for transfers between devices: 496 us -> 189 us
  local copies, waits for them, and re-layouts: 222 us -> 43.1 us
  blocking collectives: 114 us -> 0 us
  Pallas kernels: 0 us -> 76.6 us
  starting transfers between devices: 1.32 us -> 60 us
  matrix products: 189 us -> 137 us
  other arithmetic: 86.1 us -> 40 us
  between operations: 16.7 us -> 2.26 us
    all_gather x9 -> x0, waiting for transfers between devices: 244 us -> none  [the longest x1 54.1 us: local(): grad_whole = lax.all_gather(cotangent, 'heads', axis=0, tiled=True)]
    ppermute x0 -> x60, waiting for transfers between devices: none -> 189 us  [the longest x58 189 us: swap(): return lax.ppermute(value, ALL, pairs)]
    dynamic_update_slice x12 -> x0, local copies, waits for them, and re-layouts: 164 us -> none  [local(): lax.map(attend_back_row, (queries, keys, values, allowed, logsum, grad_he...]
    reduce_scatter x9 -> x0, waiting for transfers between devices: 152 us -> none  [the longest x1 52.2 us: local(): lax.psum_scatter(resid_term.astype(jnp.bfloat16), 'heads', scatter_dimens...]
    unnamed x3 -> x0, blocking collectives: 101 us -> none
    psum x1 -> x0, waiting for transfers between devices: 94.9 us -> none  [local(): lax.psum(branch.astype(jnp.bfloat16), 'heads').astype(jnp.float32)]
    pallas_call x0 -> x6, Pallas kernels: none -> 76.6 us  [the longest x1 34.3 us: attend_back(): pl.pallas_call(partial(attend_back_kernel, halo, block), grid=(heads,), o...]
    ppermute x0 -> x60, starting transfers between devices: none -> 60 us  [the longest x58 53.9 us: swap(): return lax.ppermute(value, ALL, pairs)]
  transfers between devices with their start and end apart: 19 -> 60, of which waited for: 12 -> 25; matrix products, arithmetic and copies ran while one was open for 41% -> 28% of each run, Pallas kernels for 0% -> 8%
where the time goes in v1:
time: 558 us; the launch traced here: 548 us
  waiting for transfers between devices  189 us (34%)
  matrix products  137 us (25%)
  Pallas kernels  76.6 us (14%)
  starting transfers between devices  60 us (11%)
  local copies, waits for them, and re-layouts  43.1 us (8%)
  other arithmetic  40 us (7%)
    ppermute x58, waiting for transfers between devices, swap(): return lax.ppermute(value, ALL, pairs)  189 us
    dot_general x6, matrix products, dot_nn(): lax.dot_general(left, right, (((1,), (0,)), ((), ())), preferred_element_...  59 us
    ppermute x58, starting transfers between devices, swap(): return lax.ppermute(value, ALL, pairs)  53.9 us
    dot_general x6, matrix products, dot_tn(): lax.dot_general(left, right, (((0,), (0,)), ((), ())), preferred_element_...  46.4 us
    pallas_call x1, Pallas kernels, attend_back(): pl.pallas_call(partial(attend_back_kernel, halo, block), grid=(heads,), o...  34.3 us
    dot_general x6, matrix products, dot_nt(): lax.dot_general(left, right, (((1,), (1,)), ((), ())), preferred_element_...  31.6 us
    pallas_call x1, Pallas kernels, attend(): pl.pallas_call(partial(attend_kernel, halo, block), grid=(heads,), out_sh...  24.4 us
    slice x21, local copies, waits for them, and re-layouts, fold(): send = lax.slice_in_dim(value, half, 2 * half, axis=axis)  20.5 us
  transfers between devices with their start and end apart: 60, of which 25 were waited for; matrix products, arithmetic and copies ran while one was open for 28% of the time, Pallas kernels for 8%

profile of v1, /device:TPU:0, one launch (start us, length us, event | category | flops | bytes accessed | tf_op | source)
XLA Modules:
  0.0 548.2 jit_solution(6471067283314508334)
XLA Ops:
  2.2 4.9 collective-permute-start
  31.2 4.5 shard_map.223
  44.9 4.8 shard_map.220
  55.9 9.1 %collective-permute-done.7 = bf16[2,160,640]{2,1,0:T(8,128)(2,1)S(1)} collective-permute-done((bf16[2,160,640]{2,1,0:T(8,128)(2,1)S(1)}, bf16[2,160,640]{2,1,0:T(8,128)(2,1)S(1)}, u32[]{:S(2)}, u32[]{:S(2)}) %collective-permute-start.7) | collective-permute-done | bytes 409632 | tf_op jit(solution)/shard_map/ppermute | solution.py:44
  69.3 4.5 collective-permute-done.2
  84.1 4.8 collective-permute-done.19
  91.1 15.3 %collective-permute-done.17 = bf16[320,1280]{1,0:T(8,128)(2,1)S(1)} collective-permute-done((bf16[320,1280]{1,0:T(8,128)(2,1)S(1)}, bf16[320,1280]{1,0:T(8,128)(2,1)S(1)}, u32[]{:S(2)}, u32[]{:S(2)}) %collective-permute-start.17) | collective-permute-done | bytes 819232 | tf_op jit(solution)/shard_map/ppermute | solution.py:44
  108.2 7.0 %collective-permute-done.27 = bf16[320,640]{1,0:T(8,128)(2,1)S(1)} collective-permute-done((bf16[320,640]{1,0:T(8,128)(2,1)S(1)}, bf16[320,640]{1,0:T(8,128)(2,1)S(1)}, u32[]{:S(2)}, u32[]{:S(2)}) %collective-permute-start.27) | collective-permute-done | bytes 409632 | tf_op jit(solution)/shard_map/ppermute | solution.py:44
  117.0 12.0 %collective-permute-done.20 = bf16[640,640]{1,0:T(8,128)(2,1)S(1)} collective-permute-done((bf16[640,640]{1,0:T(8,128)(2,1)S(1)}, bf16[640,640]{1,0:T(8,128)(2,1)S(1)}, u32[]{:S(2)}, u32[]{:S(2)}) %collective-permute-start.20) | collective-permute-done | bytes 819232 | tf_op jit(solution)/shard_map/ppermute | solution.py:44
  129.2 3.6 collective-permute-done.4
  134.2 12.9 %collective-permute-done.25 = bf16[320,1280]{1,0:T(8,128)(2,1)S(1)} collective-permute-done((bf16[320,1280]{1,0:T(8,128)(2,1)S(1)}, bf16[320,1280]{1,0:T(8,128)(2,1)S(1)}, u32[]{:S(2)}, u32[]{:S(2)}) %collective-permute-start.25) | collective-permute-done | bytes 819232 | tf_op jit(solution)/shard_map/ppermute | solution.py:44
  150.5 7.5 %fusion.47.k_ref = f32[1280,896]{1,0:T(8,128)} fusion(bf16[1280,896]{1,0:T(8,128)(2,1)S(1)} %multiply_convert_fusion, bf16[640,1280]{1,0:T(8,128)(2,1)S(1)} %collective-permute-done.18, bf16[320,1280]{1,0:T(8,128)(2,1)S(1)} %collective-permute-done.17, bf16[320,640]{1,0:T(8,128)(2,1)S(1)} %collective-permute-done.16, ...), kind=kOutput, calls=%fused_computation.146 | convolution fusion | flops 2949120000 | bytes 10158080 | tf_op jit(solution)/shard_map/dot_general | solution.py:141
  157.9 8.9 %fusion.45.v_ref = f32[1280,896]{1,0:T(8,128)} fusion(bf16[1280,896]{1,0:T(8,128)(2,1)S(1)} %multiply_convert_fusion, bf16[640,1280]{1,0:T(8,128)(2,1)S(1)} %collective-permute-done.21, bf16[640,640]{1,0:T(8,128)(2,1)S(1)} %collective-permute-done.20, bf16[320,640]{1,0:T(8,128)(2,1)S(1)} %collective-permute-done.19, bf16[320,640]{1,0:T(8,128)(2,1)S(1)} %get-tuple-element.45), kind=kOutput, calls=%fused_computation.144 | convolution fusion | flops 2949120000 | bytes 10158080 | tf_op jit(solution)/shard_map/dot_general | solution.py:141
  166.9 8.0 %fusion.17.q_ref = f32[1280,768]{1,0:T(8,128)} fusion(bf16[1280,896]{1,0:T(8,128)(2,1)S(1)} %multiply_convert_fusion, bf16[640,1280]{1,0:T(8,128)(2,1)S(1)} %collective-permute-done.10, bf16[640,640]{1,0:T(8,128)(2,1)S(1)} %collective-permute-done.9, bf16[320,640]{1,0:T(8,128)(2,1)S(1)} %collective-permute-done.8, bf16[320,640]{1,0:T(8,128)(2,1)S(1)} %get-tuple-element.47), kind=kOutput, calls=%fused_computation.91 | convolution fusion | flops 2529689600 | bytes 9175040 | tf_op jit(solution)/shard_map/dot_general | solution.py:141
  174.9 24.4 %shard_map.221 = (bf16[1280,768]{1,0:T(8,128)(2,1)}, bf16[1280,896]{1,0:T(8,128)(2,1)}, bf16[1280,896]{1,0:T(8,128)(2,1)}, bf16[1280,768]{1,0:T(8,128)(2,1)}, f32[16,1,768]{2,1,0:T(1,128)}) custom-call(f32[1280,768]{1,0:T(8,128)} %fusion.17.q_ref, f32[1280,896]{1,0:T(8,128)} %fusion.47.k_ref, f32[1280,896]{1,0:T(8,128)} %fusion.45.v_ref, ...), custom_call_target="tpu_custom_call" | custom-call | tf_op jit(solution)/shard_map/pallas_call | solution.py:197
  199.4 6.5 %multiply_reduce_fusion.5 = (f32[768]{0:T(1024)S(1)}, f32[1280,768]{1,0:T(8,128)S(1)}) fusion(bf16[1280,768]{1,0:T(8,128)(2,1)} %get-tuple-element.22, bf16[640,1280]{1,0:T(8,128)(2,1)} %collective-permute-done.5, bf16[320,1280]{1,0:T(8,128)(2,1)} %copy-done.31, bf16[320,640]{1,0:T(8,128)(2,1)} %copy-done.12, bf16[320,640]{1,0:T(8,128)(2,1)S(1)} %get-tuple-element.44, ...), kind=kOutput, calls=%fused_computation.38 | convolution fusion | flops 2532637952 | bytes 13110272 | tf_op jit(solution)/shard_map/dot_general | solution.py:145
  206.0 6.0 %convolution_add_fusion = f32[1280,768]{0,1:T(8,128)S(1)} fusion(f32[1280]{0:T(1024)S(1)} %add.253, bf16[640,1280]{1,0:T(8,128)(2,1)} %collective-permute-done.29, bf16[640,640]{1,0:T(8,128)(2,1)S(1)} %copy-done.34, bf16[320,640]{1,0:T(8,128)(2,1)S(1)} %copy-done.15, bf16[320,640]{1,0:T(8,128)(2,1)S(1)} %get-tuple-element.42, ...), kind=kOutput, calls=%fused_computation.39 | convolution fusion | flops 2533621760 | bytes 11154432 | tf_op jit(solution)/shard_map/dot_general | solution.py:141
  212.0 5.7 %fusion.22 = f32[1280,1280]{1,0:T(8,128)} fusion(f32[1280,768]{1,0:T(8,128)S(1)} %copy-done.4, f32[1280,768]{0,1:T(8,128)S(1)} %convolution_add_fusion), kind=kOutput, calls=%fused_computation.96 | convolution fusion | flops 2526412800 | bytes 14417920 | tf_op jit(solution)/shard_map/dot_general | solution.py:149
  217.8 9.2 %convert_reduce_fusion = (f32[1280]{0:T(1024)}, bf16[1280,768]{0,1:T(8,128)(2,1)S(1)}) fusion(f32[1280,768]{0,1:T(8,128)S(1)} %convolution_add_fusion, f32[1280,768]{1,0:T(8,128)S(1)} %copy-done.4, bf16[640,1280]{1,0:T(8,128)(2,1)} %collective-permute-done.26, bf16[320,1280]{1,0:T(8,128)(2,1)S(1)} %copy-done.30, bf16[320,640]{1,0:T(8,128)(2,1)S(1)} %copy-done.11, ...), kind=kOutput, calls=%fused_computation.29 | convolution fusion | flops 2552298240 | bytes 13112320 | tf_op jit(solution)/shard_map/dot_general | solution.py:141
  227.0 5.2 fusion.91
  232.1 11.2 %multiply_reduce_fusion.1 = (f32[1280]{0:T(1024)}, f32[768]{0:T(1024)S(1)}, f32[1280,768]{1,0:T(8,128)S(1)}) fusion(f32[1280,768]{1,0:T(8,128)S(1)} %get-tuple-element.67, f32[768]{0:T(1024)S(1)} %get-tuple-element.61, f32[1280]{0:T(1024)S(1)} %mul.241, bf16[1280,768]{0,1:T(8,128)(2,1)S(1)} %get-tuple-element.71, ...), kind=kOutput, calls=%fused_computation.27 | convolution fusion | flops 2535585792 | bytes 13123584 | tf_op jit(solution)/shard_map/dot_general | solution.py:145
  244.7 6.8 %convolution_convert_fusion.g_ref = bf16[1280,768]{1,0:T(8,128)(2,1)} fusion(f32[1280,768]{1,0:T(8,128)S(1)} %get-tuple-element.41, bf16[640,1280]{1,0:T(8,128)(2,1)} %collective-permute-done.5, bf16[320,1280]{1,0:T(8,128)(2,1)S(1)} %copy-done.32, bf16[320,640]{1,0:T(8,128)(2,1)S(1)} %copy-done.13, bf16[320,640]{1,0:T(8,128)(2,1)S(1)} %get-tuple-element.44), kind=kOutput, calls=%fused_computation.41 | convolution fusion | flops 2531655680 | bytes 9175040 | tf_op jit(solution)/shard_map/dot_general | solution.py:141
  251.5 34.3 %shard_map.224 = (bf16[1280,768]{1,0:T(8,128)(2,1)}, bf16[1280,768]{1,0:T(8,128)(2,1)}, bf16[1280,768]{1,0:T(8,128)(2,1)}, bf16[1280,128]{1,0:T(8,128)(2,1)}, bf16[1280,128]{1,0:T(8,128)(2,1)}) custom-call(bf16[1280,768]{1,0:T(8,128)(2,1)} %get-tuple-element.23.q_ref, bf16[1280,896]{1,0:T(8,128)(2,1)} %get-tuple-element.24.k_ref, ...), custom_call_target="tpu_custom_call" | custom-call | tf_op jit(solution)/shard_map/pallas_call | solution.py:255
  294.8 9.0 %add_add_fusion.1.x_ref = f32[1280,768]{1,0:T(8,128)} fusion(f32[1280,768]{1,0:T(8,128)} %copy-done.6, f32[1280]{0:T(1024)} %add.259, bf16[640,1280]{1,0:T(8,128)(2,1)} %collective-permute-done.26, bf16[320,1280]{1,0:T(8,128)(2,1)} %copy-done.29, bf16[320,640]{1,0:T(8,128)(2,1)} %copy-done.10, bf16[320,640]{1,0:T(8,128)(2,1)S(1)} %get-tuple-element.43, ...), kind=kOutput, calls=%fused_computation.35 | convolution fusion | flops 2540503040 | bytes 15078400 | tf_op jit(solution)/shard_map/dot_general | solution.py:145
  303.9 12.1 %fusion.48 = f32[1280,768]{1,0:T(8,128)} fusion(bf16[1280,768]{1,0:T(8,128)(2,1)S(1)} %copy-done.45, bf16[640,1280]{1,0:T(8,128)(2,1)S(1)} %copy-done.50, bf16[640,640]{1,0:T(8,128)(2,1)S(1)} %copy-done.28, bf16[320,640]{1,0:T(8,128)(2,1)S(1)} %collective-permute-done.8, bf16[320,640]{1,0:T(8,128)(2,1)S(1)} %get-tuple-element.47), kind=kOutput, calls=%fused_computation.147 | convolution fusion | flops 2529689600 | bytes 9175040 | tf_op jit(solution)/shard_map/dot_general | solution.py:145
  316.0 4.6 fusion.19
  323.1 5.3 fusion.46
  328.5 14.8 %multiply_reduce_fusion.2 = (f32[1280]{0:T(1024)S(1)}, f32[768]{0:T(1024)S(1)}, f32[1280,768]{1,0:T(8,128)}) fusion(f32[1280,896]{1,0:T(8,128)} %shard_map.220, f32[768]{0:T(1024)S(1)} %copy-done.37, f32[1280]{0:T(1024)S(1)} %mul.229, f32[2560,64]{1,0:T(8,128)S(1)} %bitcast.110, bf16[1280,768]{1,0:T(8,128)(2,1)S(1)} %copy-done.41, ...), kind=kOutput, calls=%fused_computation.28 | convolution fusion | flops 2540500992 | bytes 21643264 | tf_op jit(solution)/shard_map/dot_general | solution.py:145
  345.0 3.4 collective-permute-start.55
  348.5 6.3 %fusion.15 = f32[1280,1280]{1,0:T(8,128)} fusion(bf16[1280,768]{1,0:T(8,128)(2,1)} %get-tuple-element.27, bf16[1280,896]{1,0:T(8,128)(2,1)S(1)} %copy-done.9), kind=kOutput, calls=%fused_computation.89 | convolution fusion | flops 2516582400 | bytes 10485760 | tf_op jit(solution)/shard_map/dot_general | solution.py:149
  354.8 4.3 shard_map.222
  359.0 3.4 slice.628
  362.5 3.4 slice.626
  366.4 3.5 slice.624
  382.1 4.8 fusion.13
  386.9 3.7 collective-permute-start.59
  390.6 5.0 fusion.11
  395.6 4.2 shard_map.225
  422.9 7.9 %collective-permute-done.32 = bf16[640,640]{1,0:T(8,128)(2,1)} collective-permute-done((bf16[640,640]{1,0:T(8,128)(2,1)}, bf16[640,640]{1,0:T(8,128)(2,1)}, u32[]{:S(2)}, u32[]{:S(2)}) %collective-permute-start.32) | collective-permute-done | bytes 819232 | tf_op jit(solution)/shard_map/ppermute | solution.py:44
  432.7 15.6 %collective-permute-done.40 = bf16[640,640]{1,0:T(8,128)(2,1)} collective-permute-done((bf16[640,640]{1,0:T(8,128)(2,1)}, bf16[640,640]{1,0:T(8,128)(2,1)}, u32[]{:S(2)}, u32[]{:S(2)}) %collective-permute-start.40) | collective-permute-done | bytes 819232 | tf_op jit(solution)/shard_map/ppermute | solution.py:44
  450.3 14.8 %collective-permute-done.48 = bf16[640,640]{1,0:T(8,128)(2,1)} collective-permute-done((bf16[640,640]{1,0:T(8,128)(2,1)S(1)}, bf16[640,640]{1,0:T(8,128)(2,1)}, u32[]{:S(2)}, u32[]{:S(2)}) %collective-permute-start.48) | collective-permute-done | bytes 819232 | tf_op jit(solution)/shard_map/ppermute | solution.py:44
  469.3 5.4 collective-permute-done.43
  476.9 22.8 %collective-permute-done.49 = bf16[320,640]{1,0:T(8,128)(2,1)S(1)} collective-permute-done((bf16[320,640]{1,0:T(8,128)(2,1)S(1)}, bf16[320,640]{1,0:T(8,128)(2,1)S(1)}, u32[]{:S(2)}, u32[]{:S(2)}) %collective-permute-start.49) | collective-permute-done | bytes 409632 | tf_op jit(solution)/shard_map/ppermute | solution.py:44
  504.1 12.1 %collective-permute-done.53 = bf16[2,160,640]{2,1,0:T(8,128)(2,1)S(1)} collective-permute-done((bf16[2,160,640]{2,1,0:T(8,128)(2,1)S(1)}, bf16[2,160,640]{2,1,0:T(8,128)(2,1)S(1)}, u32[]{:S(2)}, u32[]{:S(2)}) %collective-permute-start.53) | collective-permute-done | bytes 409632 | tf_op jit(solution)/shard_map/ppermute | solution.py:44
  516.9 8.3 %collective-permute-done.54 = bf16[2,80,640]{2,1,0:T(8,128)(2,1)S(1)} collective-permute-done((bf16[2,80,640]{2,1,0:T(8,128)(2,1)S(1)}, bf16[2,80,640]{2,1,0:T(8,128)(2,1)S(1)}, u32[]{:S(2)}, u32[]{:S(2)}) %collective-permute-start.54) | collective-permute-done | bytes 204832 | tf_op jit(solution)/shard_map/ppermute | solution.py:44
  526.0 3.3 collective-permute-done.37
  529.6 6.4 %collective-permute-done.45 = bf16[2,160,640]{2,1,0:T(8,128)(2,1)S(1)} collective-permute-done((bf16[2,160,640]{2,1,0:T(8,128)(2,1)S(1)}, bf16[2,160,640]{2,1,0:T(8,128)(2,1)S(1)}, u32[]{:S(2)}, u32[]{:S(2)}) %collective-permute-start.45) | collective-permute-done | bytes 409632 | tf_op jit(solution)/shard_map/ppermute | solution.py:44
  536.2 8.0 %collective-permute-done.38 = bf16[2,80,640]{2,1,0:T(8,128)(2,1)S(1)} collective-permute-done((bf16[2,80,640]{2,1,0:T(8,128)(2,1)S(1)}, bf16[2,80,640]{2,1,0:T(8,128)(2,1)S(1)}, u32[]{:S(2)}, u32[]{:S(2)}) %collective-permute-start.38) | collective-permute-done | bytes 204832 | tf_op jit(solution)/shard_map/ppermute | solution.py:44
  (409 shorter events, 136.3 us)
Async XLA Ops:
  2.2 40.8 %collective-permute-start = (bf16[64,1280]{1,0:T(8,128)(2,1)}, bf16[64,1280]{1,0:T(8,128)(2,1)S(1)}, u32[]{:S(2)}, u32[]{:S(2)}) collective-permute-start(bf16[64,1280]{1,0:T(8,128)(2,1)} %slice.302), channel_id=1, source_target_pairs={{0,1},{2,3},{4,5},{6,7},{8,9},{10,11},{12,13},{14,15},{16,17},{18,... | collective-permute-start | bytes 491528 | tf_op jit(solution)/shard_map/ppermute | solution.py:305
  9.0 43.6 %collective-permute-start.6 = (bf16[2,80,640]{2,1,0:T(8,128)(2,1)S(1)}, bf16[2,80,640]{2,1,0:T(8,128)(2,1)S(1)}, u32[]{:S(2)}, u32[]{:S(2)}) collective-permute-start(bf16[2,80,640]{2,1,0:T(8,128)(2,1)S(1)} %pad_maximum_fusion.44), channel_id=1, source_target_pairs={{0,16},{1,17},{2,18},{3,19},{4,20},{5,21},{6,22},{7,23},{8,24},{9,... | collective-permute-start | bytes 614408 | tf_op jit(solution)/shard_map/ppermute | solution.py:44
  12.6 41.9 %collective-permute-start.1 = (bf16[2,80,640]{2,1,0:T(8,128)(2,1)S(1)}, bf16[2,80,640]{2,1,0:T(8,128)(2,1)S(1)}, u32[]{:S(2)}, u32[]{:S(2)}) collective-permute-start(bf16[2,80,640]{2,1,0:T(8,128)(2,1)S(1)} %pad_maximum_fusion.43), channel_id=1, source_target_pairs={{0,16},{1,17},{2,18},{3,19},{4,20},{5,21},{6,22},{7,23},{8,24},{9,... | collective-permute-start | bytes 614408 | tf_op jit(solution)/shard_map/ppermute | solution.py:44
  14.0 53.0 %collective-permute-start.22 = (bf16[2,80,640]{2,1,0:T(8,128)(2,1)S(1)}, bf16[2,80,640]{2,1,0:T(8,128)(2,1)S(1)}, u32[]{:S(2)}, u32[]{:S(2)}) collective-permute-start(bf16[2,80,640]{2,1,0:T(8,128)(2,1)S(1)} %pad_maximum_fusion.45), channel_id=1, source_target_pairs={{0,16},{1,17},{2,18},{3,19},{4,20},{5,21},{6,22},{7,23},{8,24},{9,... | collective-permute-start | bytes 614408 | tf_op jit(solution)/shard_map/ppermute | solution.py:44
  54.5 19.3 %collective-permute-start.2 = (bf16[2,160,640]{2,1,0:T(8,128)(2,1)S(1)}, bf16[2,160,640]{2,1,0:T(8,128)(2,1)S(1)}, u32[]{:S(2)}, u32[]{:S(2)}) collective-permute-start(bf16[2,160,640]{2,1,0:T(8,128)(2,1)S(1)} %pad_maximum_fusion.40), channel_id=1, source_target_pairs={{0,8},{1,9},{2,10},{3,11},{4,12},{5,13},{6,14},{7,15},{8,0},{9,1},... | collective-permute-start | bytes 1228808 | tf_op jit(solution)/shard_map/ppermute | solution.py:44
  67.0 13.6 %collective-permute-start.23 = (bf16[2,160,640]{2,1,0:T(8,128)(2,1)S(1)}, bf16[2,160,640]{2,1,0:T(8,128)(2,1)S(1)}, u32[]{:S(2)}, u32[]{:S(2)}) collective-permute-start(bf16[2,160,640]{2,1,0:T(8,128)(2,1)S(1)} %pad_maximum_fusion.42), channel_id=1, source_target_pairs={{0,8},{1,9},{2,10},{3,11},{4,12},{5,13},{6,14},{7,15},{8,0},{9,1},... | collective-permute-start | bytes 1228808 | tf_op jit(solution)/shard_map/ppermute | solution.py:44
  67.8 14.8 %collective-permute-start.8 = (bf16[320,640]{1,0:T(8,128)(2,1)S(1)}, bf16[320,640]{1,0:T(8,128)(2,1)S(1)}, u32[]{:S(2)}, u32[]{:S(2)}) collective-permute-start(bf16[320,640]{1,0:T(8,128)(2,1)S(1)} %get-tuple-element.47), channel_id=1, source_target_pairs={{0,4},{1,5},{2,6},{3,7},{4,0},{5,1},{6,2},{7,3},{8,12},{9,13},{10,... | collective-permute-start | bytes 1228808 | tf_op jit(solution)/shard_map/ppermute | solution.py:44
  74.0 14.9 %collective-permute-start.19 = (bf16[320,640]{1,0:T(8,128)(2,1)S(1)}, bf16[320,640]{1,0:T(8,128)(2,1)S(1)}, u32[]{:S(2)}, u32[]{:S(2)}) collective-permute-start(bf16[320,640]{1,0:T(8,128)(2,1)S(1)} %get-tuple-element.45), channel_id=1, source_target_pairs={{0,4},{1,5},{2,6},{3,7},{4,0},{5,1},{6,2},{7,3},{8,12},{9,13},{10,... | collective-permute-start | bytes 1228808 | tf_op jit(solution)/shard_map/ppermute | solution.py:44
  75.5 13.5 %collective-permute-start.3 = (bf16[320,640]{1,0:T(8,128)(2,1)S(1)}, bf16[320,640]{1,0:T(8,128)(2,1)S(1)}, u32[]{:S(2)}, u32[]{:S(2)}) collective-permute-start(bf16[320,640]{1,0:T(8,128)(2,1)S(1)} %get-tuple-element.44), channel_id=1, source_target_pairs={{0,1},{1,0},{2,3},{3,2},{4,5},{5,4},{6,7},{7,6},{8,9},{9,8},{10,11... | collective-permute-start | bytes 1228808 | tf_op jit(solution)/shard_map/ppermute | solution.py:44
  77.3 29.1 %collective-permute-start.17 = (bf16[320,1280]{1,0:T(8,128)(2,1)S(1)}, bf16[320,1280]{1,0:T(8,128)(2,1)S(1)}, u32[]{:S(2)}, u32[]{:S(2)}) collective-permute-start(bf16[320,1280]{1,0:T(8,128)(2,1)S(1)} %pad_maximum_fusion.20), channel_id=1, source_target_pairs={{0,4},{1,5},{2,6},{3,7},{4,0},{5,1},{6,2},{7,3},{8,12},{9,13},{10,... | collective-permute-start | bytes 2457608 | tf_op jit(solution)/shard_map/ppermute | solution.py:44
  80.8 27.3 %collective-permute-start.24 = (bf16[320,640]{1,0:T(8,128)(2,1)S(1)}, bf16[320,640]{1,0:T(8,128)(2,1)S(1)}, u32[]{:S(2)}, u32[]{:S(2)}) collective-permute-start(bf16[320,640]{1,0:T(8,128)(2,1)S(1)} %get-tuple-element.43), channel_id=1, source_target_pairs={{0,1},{1,0},{2,3},{3,2},{4,5},{5,4},{6,7},{7,6},{8,9},{9,8},{10,11... | collective-permute-start | bytes 1228808 | tf_op jit(solution)/shard_map/ppermute | solution.py:44
  82.6 32.7 %collective-permute-start.27 = (bf16[320,640]{1,0:T(8,128)(2,1)S(1)}, bf16[320,640]{1,0:T(8,128)(2,1)S(1)}, u32[]{:S(2)}, u32[]{:S(2)}) collective-permute-start(bf16[320,640]{1,0:T(8,128)(2,1)S(1)} %get-tuple-element.42), channel_id=1, source_target_pairs={{0,4},{1,5},{2,6},{3,7},{4,0},{5,1},{6,2},{7,3},{8,12},{9,13},{10,... | collective-permute-start | bytes 1228808 | tf_op jit(solution)/shard_map/ppermute | solution.py:44
  88.9 27.9 %collective-permute-start.9 = (bf16[640,640]{1,0:T(8,128)(2,1)S(1)}, bf16[640,640]{1,0:T(8,128)(2,1)S(1)}, u32[]{:S(2)}, u32[]{:S(2)}) collective-permute-start(bf16[640,640]{1,0:T(8,128)(2,1)S(1)} %pad_maximum_fusion.19), channel_id=1, source_target_pairs={{0,1},{1,0},{2,3},{3,2},{4,5},{5,4},{6,7},{7,6},{8,9},{9,8},{10,11... | collective-permute-start | bytes 2457608 | tf_op jit(solution)/shard_map/ppermute | solution.py:44
  89.0 40.0 %collective-permute-start.20 = (bf16[640,640]{1,0:T(8,128)(2,1)S(1)}, bf16[640,640]{1,0:T(8,128)(2,1)S(1)}, u32[]{:S(2)}, u32[]{:S(2)}) collective-permute-start(bf16[640,640]{1,0:T(8,128)(2,1)S(1)} %pad_maximum_fusion.21), channel_id=1, source_target_pairs={{0,1},{1,0},{2,3},{3,2},{4,5},{5,4},{6,7},{7,6},{8,9},{9,8},{10,11... | collective-permute-start | bytes 2457608 | tf_op jit(solution)/shard_map/ppermute | solution.py:44
  106.4 26.3 %collective-permute-start.4 = (bf16[320,1280]{1,0:T(8,128)(2,1)S(1)}, bf16[320,1280]{1,0:T(8,128)(2,1)S(1)}, u32[]{:S(2)}, u32[]{:S(2)}) collective-permute-start(bf16[320,1280]{1,0:T(8,128)(2,1)S(1)} %pad_maximum_fusion.17), channel_id=1, source_target_pairs={{0,4},{1,5},{2,6},{3,7},{4,0},{5,1},{6,2},{7,3},{8,12},{9,13},{10,... | collective-permute-start | bytes 2457608 | tf_op jit(solution)/shard_map/ppermute | solution.py:44
  108.1 42.1 %collective-permute-start.18 = (bf16[640,1280]{1,0:T(8,128)(2,1)S(1)}, bf16[640,1280]{1,0:T(8,128)(2,1)S(1)}, u32[]{:S(2)}, u32[]{:S(2)}) collective-permute-start(bf16[640,1280]{1,0:T(8,128)(2,1)S(1)} %pad_maximum_fusion.9), channel_id=1, source_target_pairs={{0,2},{1,3},{2,0},{3,1},{4,6},{5,7},{6,4},{7,5},{8,10},{9,11},{10,... | collective-permute-start | bytes 4915208 | tf_op jit(solution)/shard_map/ppermute | solution.py:44
  115.2 31.8 %collective-permute-start.25 = (bf16[320,1280]{1,0:T(8,128)(2,1)S(1)}, bf16[320,1280]{1,0:T(8,128)(2,1)S(1)}, u32[]{:S(2)}, u32[]{:S(2)}) collective-permute-start(bf16[320,1280]{1,0:T(8,128)(2,1)S(1)} %pad_maximum_fusion.23), channel_id=1, source_target_pairs={{0,4},{1,5},{2,6},{3,7},{4,0},{5,1},{6,2},{7,3},{8,12},{9,13},{10,... | collective-permute-start | bytes 2457608 | tf_op jit(solution)/shard_map/ppermute | solution.py:44
  116.8 31.7 %collective-permute-start.28 = (bf16[640,640]{1,0:T(8,128)(2,1)S(1)}, bf16[640,640]{1,0:T(8,128)(2,1)S(1)}, u32[]{:S(2)}, u32[]{:S(2)}) collective-permute-start(bf16[640,640]{1,0:T(8,128)(2,1)S(1)} %pad_maximum_fusion.24), channel_id=1, source_target_pairs={{0,1},{1,0},{2,3},{3,2},{4,5},{5,4},{6,7},{7,6},{8,9},{9,8},{10,11... | collective-permute-start | bytes 2457608 | tf_op jit(solution)/shard_map/ppermute | solution.py:44
  129.0 37.9 %collective-permute-start.10 = (bf16[640,1280]{1,0:T(8,128)(2,1)S(1)}, bf16[640,1280]{1,0:T(8,128)(2,1)S(1)}, u32[]{:S(2)}, u32[]{:S(2)}) collective-permute-start(bf16[640,1280]{1,0:T(8,128)(2,1)S(1)} %pad_maximum_fusion.8), channel_id=1, source_target_pairs={{0,2},{1,3},{2,0},{3,1},{4,6},{5,7},{6,4},{7,5},{8,10},{9,11},{10,... | collective-permute-start | bytes 4915208 | tf_op jit(solution)/shard_map/ppermute | solution.py:44
  132.8 25.1 %collective-permute-start.21 = (bf16[640,1280]{1,0:T(8,128)(2,1)S(1)}, bf16[640,1280]{1,0:T(8,128)(2,1)S(1)}, u32[]{:S(2)}, u32[]{:S(2)}) collective-permute-start(bf16[640,1280]{1,0:T(8,128)(2,1)S(1)} %pad_maximum_fusion.10), channel_id=1, source_target_pairs={{0,2},{1,3},{2,0},{3,1},{4,6},{5,7},{6,4},{7,5},{8,10},{9,11},{10,... | collective-permute-start | bytes 4915208 | tf_op jit(solution)/shard_map/ppermute | solution.py:44
  147.0 52.3 %collective-permute-start.5 = (bf16[640,1280]{1,0:T(8,128)(2,1)}, bf16[640,1280]{1,0:T(8,128)(2,1)}, u32[]{:S(2)}, u32[]{:S(2)}) collective-permute-start(bf16[640,1280]{1,0:T(8,128)(2,1)} %pad_maximum_fusion.7), channel_id=1, source_target_pairs={{0,2},{1,3},{2,0},{3,1},{4,6},{5,7},{6,4},{7,5},{8,10},{9,11},{10,... | collective-permute-start | bytes 4915208 | tf_op jit(solution)/shard_map/ppermute | solution.py:44
  148.5 69.2 %collective-permute-start.26 = (bf16[640,1280]{1,0:T(8,128)(2,1)}, bf16[640,1280]{1,0:T(8,128)(2,1)}, u32[]{:S(2)}, u32[]{:S(2)}) collective-permute-start(bf16[640,1280]{1,0:T(8,128)(2,1)} %pad_maximum_fusion.11), channel_id=1, source_target_pairs={{0,2},{1,3},{2,0},{3,1},{4,6},{5,7},{6,4},{7,5},{8,10},{9,11},{10,... | collective-permute-start | bytes 4915208 | tf_op jit(solution)/shard_map/ppermute | solution.py:44
  150.2 55.7 %collective-permute-start.29 = (bf16[640,1280]{1,0:T(8,128)(2,1)}, bf16[640,1280]{1,0:T(8,128)(2,1)}, u32[]{:S(2)}, u32[]{:S(2)}) collective-permute-start(bf16[640,1280]{1,0:T(8,128)(2,1)} %pad_maximum_fusion.12), channel_id=1, source_target_pairs={{0,2},{1,3},{2,0},{3,1},{4,6},{5,7},{6,4},{7,5},{8,10},{9,11},{10,... | collective-permute-start | bytes 4915208 | tf_op jit(solution)/shard_map/ppermute | solution.py:44
  289.2 31.5 %collective-permute-start.30 = (bf16[2560,64]{0,1:T(8,128)(2,1)}, bf16[2560,64]{0,1:T(8,128)(2,1)}, u32[]{:S(2)}, u32[]{:S(2)}) collective-permute-start(bf16[2560,64]{0,1:T(8,128)(2,1)} %copy.47), channel_id=1, source_target_pairs={{1,0},{3,2},{5,4},{7,6},{9,8},{11,10},{13,12},{15,14},{17,16},{19,... | collective-permute-start | bytes 983048 | tf_op jit(solution)/shard_map/ppermute | solution.py:359
  345.0 28.7 %collective-permute-start.55 = (f32[16,160]{1,0:T(8,128)S(1)}, f32[16,160]{1,0:T(8,128)S(1)}, u32[]{:S(2)}, u32[]{:S(2)}) collective-permute-start(f32[16,160]{1,0:T(8,128)S(1)} %slice.481), channel_id=1, source_target_pairs={{0,16},{1,17},{2,18},{3,19},{4,20},{5,21},{6,22},{7,23},{8,24},{9,... | collective-permute-start | bytes 30728 | tf_op jit(solution)/shard_map/ppermute | solution.py:44
  362.4 42.6 %collective-permute-start.31 = (bf16[640,1280]{1,0:T(8,128)(2,1)}, bf16[640,1280]{1,0:T(8,128)(2,1)}, u32[]{:S(2)}, u32[]{:S(2)}) collective-permute-start(bf16[640,1280]{1,0:T(8,128)(2,1)} %slice.628), channel_id=1, source_target_pairs={{0,2},{1,3},{2,0},{3,1},{4,6},{5,7},{6,4},{7,5},{8,10},{9,11},{10,... | collective-permute-start | bytes 4915208 | tf_op jit(solution)/shard_map/ppermute | solution.py:44
  365.9 43.4 %collective-permute-start.39 = (bf16[640,1280]{1,0:T(8,128)(2,1)}, bf16[640,1280]{1,0:T(8,128)(2,1)}, u32[]{:S(2)}, u32[]{:S(2)}) collective-permute-start(bf16[640,1280]{1,0:T(8,128)(2,1)} %slice.626), channel_id=1, source_target_pairs={{0,2},{1,3},{2,0},{3,1},{4,6},{5,7},{6,4},{7,5},{8,10},{9,11},{10,... | collective-permute-start | bytes 4915208 | tf_op jit(solution)/shard_map/ppermute | solution.py:44
  369.9 42.3 %collective-permute-start.47 = (bf16[640,1280]{1,0:T(8,128)(2,1)}, bf16[640,1280]{1,0:T(8,128)(2,1)}, u32[]{:S(2)}, u32[]{:S(2)}) collective-permute-start(bf16[640,1280]{1,0:T(8,128)(2,1)} %slice.624), channel_id=1, source_target_pairs={{0,2},{1,3},{2,0},{3,1},{4,6},{5,7},{6,4},{7,5},{8,10},{9,11},{10,... | collective-permute-start | bytes 4915208 | tf_op jit(solution)/shard_map/ppermute | solution.py:44
  373.2 43.1 %collective-permute-start.50 = (bf16[640,1280]{1,0:T(8,128)(2,1)}, bf16[640,1280]{1,0:T(8,128)(2,1)}, u32[]{:S(2)}, u32[]{:S(2)}) collective-permute-start(bf16[640,1280]{1,0:T(8,128)(2,1)} %slice.623), channel_id=1, source_target_pairs={{0,2},{1,3},{2,0},{3,1},{4,6},{5,7},{6,4},{7,5},{8,10},{9,11},{10,... | collective-permute-start | bytes 4915208 | tf_op jit(solution)/shard_map/ppermute | solution.py:44
  386.9 17.2 %collective-permute-start.59 = (f32[1,160]{1,0:T(1,128)S(1)}, f32[1,160]{1,0:T(1,128)S(1)}, u32[]{:S(2)}, u32[]{:S(2)}) collective-permute-start(f32[1,160]{1,0:T(1,128)S(1)} %slice.489), channel_id=1, source_target_pairs={{0,1},{1,0},{2,3},{3,2},{4,5},{5,4},{6,7},{7,6},{8,9},{9,8},{10,11... | collective-permute-start | bytes 1928 | tf_op jit(solution)/shard_map/ppermute | solution.py:44
  404.2 14.2 %collective-permute-start.34 = (bf16[640,1280]{1,0:T(8,128)(2,1)S(1)}, bf16[640,1280]{1,0:T(8,128)(2,1)S(1)}, u32[]{:S(2)}, u32[]{:S(2)}) collective-permute-start(bf16[640,1280]{1,0:T(8,128)(2,1)S(1)} %slice.627), channel_id=1, source_target_pairs={{0,2},{1,3},{2,0},{3,1},{4,6},{5,7},{6,4},{7,5},{8,10},{9,11},{10,... | collective-permute-start | bytes 4915208 | tf_op jit(solution)/shard_map/ppermute | solution.py:44
  405.0 14.5 %collective-permute-start.42 = (bf16[640,1280]{1,0:T(8,128)(2,1)S(1)}, bf16[640,1280]{1,0:T(8,128)(2,1)}, u32[]{:S(2)}, u32[]{:S(2)}) collective-permute-start(bf16[640,1280]{1,0:T(8,128)(2,1)S(1)} %slice.625), channel_id=1, source_target_pairs={{0,2},{1,3},{2,0},{3,1},{4,6},{5,7},{6,4},{7,5},{8,10},{9,11},{10,... | collective-permute-start | bytes 4915208 | tf_op jit(solution)/shard_map/ppermute | solution.py:44
  409.3 21.4 %collective-permute-start.32 = (bf16[640,640]{1,0:T(8,128)(2,1)}, bf16[640,640]{1,0:T(8,128)(2,1)}, u32[]{:S(2)}, u32[]{:S(2)}) collective-permute-start(bf16[640,640]{1,0:T(8,128)(2,1)} %slice.634), channel_id=1, source_target_pairs={{0,1},{1,0},{2,3},{3,2},{4,5},{5,4},{6,7},{7,6},{8,9},{9,8},{10,11... | collective-permute-start | bytes 2457608 | tf_op jit(solution)/shard_map/ppermute | solution.py:44
  412.2 36.1 %collective-permute-start.40 = (bf16[640,640]{1,0:T(8,128)(2,1)}, bf16[640,640]{1,0:T(8,128)(2,1)}, u32[]{:S(2)}, u32[]{:S(2)}) collective-permute-start(bf16[640,640]{1,0:T(8,128)(2,1)} %slice.632), channel_id=1, source_target_pairs={{0,1},{1,0},{2,3},{3,2},{4,5},{5,4},{6,7},{7,6},{8,9},{9,8},{10,11... | collective-permute-start | bytes 2457608 | tf_op jit(solution)/shard_map/ppermute | solution.py:44
  416.3 48.8 %collective-permute-start.48 = (bf16[640,640]{1,0:T(8,128)(2,1)S(1)}, bf16[640,640]{1,0:T(8,128)(2,1)}, u32[]{:S(2)}, u32[]{:S(2)}) collective-permute-start(bf16[640,640]{1,0:T(8,128)(2,1)S(1)} %slice.630), channel_id=1, source_target_pairs={{0,1},{1,0},{2,3},{3,2},{4,5},{5,4},{6,7},{7,6},{8,9},{9,8},{10,11... | collective-permute-start | bytes 2457608 | tf_op jit(solution)/shard_map/ppermute | solution.py:44
  418.4 48.7 %collective-permute-start.51 = (bf16[320,1280]{1,0:T(8,128)(2,1)S(1)}, bf16[320,1280]{1,0:T(8,128)(2,1)S(1)}, u32[]{:S(2)}, u32[]{:S(2)}) collective-permute-start(bf16[320,1280]{1,0:T(8,128)(2,1)S(1)} %slice.629), channel_id=1, source_target_pairs={{0,4},{1,5},{2,6},{3,7},{4,0},{5,1},{6,2},{7,3},{8,12},{9,13},{10,... | collective-permute-start | bytes 2457608 | tf_op jit(solution)/shard_map/ppermute | solution.py:44
  419.5 49.2 %collective-permute-start.35 = (bf16[320,1280]{1,0:T(8,128)(2,1)S(1)}, bf16[320,1280]{1,0:T(8,128)(2,1)S(1)}, u32[]{:S(2)}, u32[]{:S(2)}) collective-permute-start(bf16[320,1280]{1,0:T(8,128)(2,1)S(1)} %slice.633), channel_id=1, source_target_pairs={{0,4},{1,5},{2,6},{3,7},{4,0},{5,1},{6,2},{7,3},{8,12},{9,13},{10,... | collective-permute-start | bytes 2457608 | tf_op jit(solution)/shard_map/ppermute | solution.py:44
  430.8 43.9 %collective-permute-start.43 = (bf16[320,1280]{1,0:T(8,128)(2,1)S(1)}, bf16[320,1280]{1,0:T(8,128)(2,1)S(1)}, u32[]{:S(2)}, u32[]{:S(2)}) collective-permute-start(bf16[320,1280]{1,0:T(8,128)(2,1)S(1)} %slice.631), channel_id=1, source_target_pairs={{0,4},{1,5},{2,6},{3,7},{4,0},{5,1},{6,2},{7,3},{8,12},{9,13},{10,... | collective-permute-start | bytes 2457608 | tf_op jit(solution)/shard_map/ppermute | solution.py:44
  448.3 53.9 %collective-permute-start.33 = (bf16[320,640]{1,0:T(8,128)(2,1)S(1)}, bf16[320,640]{1,0:T(8,128)(2,1)S(1)}, u32[]{:S(2)}, u32[]{:S(2)}) collective-permute-start(bf16[320,640]{1,0:T(8,128)(2,1)S(1)} %slice.640), channel_id=1, source_target_pairs={{0,4},{1,5},{2,6},{3,7},{4,0},{5,1},{6,2},{7,3},{8,12},{9,13},{10,... | collective-permute-start | bytes 1228808 | tf_op jit(solution)/shard_map/ppermute | solution.py:44
  465.1 37.2 %collective-permute-start.41 = (bf16[320,640]{1,0:T(8,128)(2,1)S(1)}, bf16[320,640]{1,0:T(8,128)(2,1)S(1)}, u32[]{:S(2)}, u32[]{:S(2)}) collective-permute-start(bf16[320,640]{1,0:T(8,128)(2,1)S(1)} %slice.638), channel_id=1, source_target_pairs={{0,4},{1,5},{2,6},{3,7},{4,0},{5,1},{6,2},{7,3},{8,12},{9,13},{10,... | collective-permute-start | bytes 1228808 | tf_op jit(solution)/shard_map/ppermute | solution.py:44
  467.1 32.6 %collective-permute-start.49 = (bf16[320,640]{1,0:T(8,128)(2,1)S(1)}, bf16[320,640]{1,0:T(8,128)(2,1)S(1)}, u32[]{:S(2)}, u32[]{:S(2)}) collective-permute-start(bf16[320,640]{1,0:T(8,128)(2,1)S(1)} %slice.636), channel_id=1, source_target_pairs={{0,4},{1,5},{2,6},{3,7},{4,0},{5,1},{6,2},{7,3},{8,12},{9,13},{10,... | collective-permute-start | bytes 1228808 | tf_op jit(solution)/shard_map/ppermute | solution.py:44
  468.7 32.7 %collective-permute-start.52 = (bf16[320,640]{1,0:T(8,128)(2,1)S(1)}, bf16[320,640]{1,0:T(8,128)(2,1)S(1)}, u32[]{:S(2)}, u32[]{:S(2)}) collective-permute-start(bf16[320,640]{1,0:T(8,128)(2,1)S(1)} %slice.635), channel_id=1, source_target_pairs={{0,1},{1,0},{2,3},{3,2},{4,5},{5,4},{6,7},{7,6},{8,9},{9,8},{10,11... | collective-permute-start | bytes 1228808 | tf_op jit(solution)/shard_map/ppermute | solution.py:44
  474.7 27.7 %collective-permute-start.36 = (bf16[320,640]{1,0:T(8,128)(2,1)S(1)}, bf16[320,640]{1,0:T(8,128)(2,1)S(1)}, u32[]{:S(2)}, u32[]{:S(2)}) collective-permute-start(bf16[320,640]{1,0:T(8,128)(2,1)S(1)} %slice.639), channel_id=1, source_target_pairs={{0,1},{1,0},{2,3},{3,2},{4,5},{5,4},{6,7},{7,6},{8,9},{9,8},{10,11... | collective-permute-start | bytes 1228808 | tf_op jit(solution)/shard_map/ppermute | solution.py:44
  499.6 16.7 %collective-permute-start.44 = (bf16[320,640]{1,0:T(8,128)(2,1)S(1)}, bf16[320,640]{1,0:T(8,128)(2,1)S(1)}, u32[]{:S(2)}, u32[]{:S(2)}) collective-permute-start(bf16[320,640]{1,0:T(8,128)(2,1)S(1)} %slice.637), channel_id=1, source_target_pairs={{0,1},{1,0},{2,3},{3,2},{4,5},{5,4},{6,7},{7,6},{8,9},{9,8},{10,11... | collective-permute-start | bytes 1228808 | tf_op jit(solution)/shard_map/ppermute | solution.py:44
  501.6 14.6 %collective-permute-start.53 = (bf16[2,160,640]{2,1,0:T(8,128)(2,1)S(1)}, bf16[2,160,640]{2,1,0:T(8,128)(2,1)S(1)}, u32[]{:S(2)}, u32[]{:S(2)}) collective-permute-start(bf16[2,160,640]{2,1,0:T(8,128)(2,1)S(1)} %fusion.34), channel_id=1, source_target_pairs={{0,8},{1,9},{2,10},{3,11},{4,12},{5,13},{6,14},{7,15},{8,0},{9,1},... | collective-permute-start | bytes 1228808 | tf_op jit(solution)/shard_map/ppermute | solution.py:44
  502.5 26.8 %collective-permute-start.37 = (bf16[2,160,640]{2,1,0:T(8,128)(2,1)S(1)}, bf16[2,160,640]{2,1,0:T(8,128)(2,1)S(1)}, u32[]{:S(2)}, u32[]{:S(2)}) collective-permute-start(bf16[2,160,640]{2,1,0:T(8,128)(2,1)S(1)} %fusion.40), channel_id=1, source_target_pairs={{0,8},{1,9},{2,10},{3,11},{4,12},{5,13},{6,14},{7,15},{8,0},{9,1},... | collective-permute-start | bytes 1228808 | tf_op jit(solution)/shard_map/ppermute | solution.py:44
  516.5 19.5 %collective-permute-start.45 = (bf16[2,160,640]{2,1,0:T(8,128)(2,1)S(1)}, bf16[2,160,640]{2,1,0:T(8,128)(2,1)S(1)}, u32[]{:S(2)}, u32[]{:S(2)}) collective-permute-start(bf16[2,160,640]{2,1,0:T(8,128)(2,1)S(1)} %fusion.37), channel_id=1, source_target_pairs={{0,8},{1,9},{2,10},{3,11},{4,12},{5,13},{6,14},{7,15},{8,0},{9,1},... | collective-permute-start | bytes 1228808 | tf_op jit(solution)/shard_map/ppermute | solution.py:44
  529.4 14.8 %collective-permute-start.38 = (bf16[2,80,640]{2,1,0:T(8,128)(2,1)S(1)}, bf16[2,80,640]{2,1,0:T(8,128)(2,1)S(1)}, u32[]{:S(2)}, u32[]{:S(2)}) collective-permute-start(bf16[2,80,640]{2,1,0:T(8,128)(2,1)S(1)} %slice.643), channel_id=1, source_target_pairs={{0,16},{1,17},{2,18},{3,19},{4,20},{5,21},{6,22},{7,23},{8,24},{9,... | collective-permute-start | bytes 614408 | tf_op jit(solution)/shard_map/ppermute | solution.py:44
  (77 other events, 953.3 us)
